TPU v7x, 768 devices: a whole 4x8x12 slice. The times are simulated.
768 devices in a mesh: lat: 48 (over y_hi, z, core), lon: 16 (over x, y_lo).
Axes of the slice: x: 4, y: 8 (y_hi: 2, y_lo: 4; y = y_hi * 4 + y_lo), z: 12, core: 2. Of those that a mesh axis runs over, the one named last changes fastest.
Arguments:
- fields: bfloat16 [288, 384, 384], P('lat', 'lon'), may hold values from -6 to 6
- norm_gain: float32 [192], replicated, may hold values from 0.1 to 1.9
- project_in: bfloat16 [192, 576], replicated, may hold values from -0.4375 to 0.4375
- project_out: bfloat16 [192, 192], replicated, may hold values from -0.4375 to 0.4375
- bias_table: float32 [48, 6, 144, 23], P('lat', None, 'lon'), may hold values from -4 to 400, as said below
- pad_rows: int32 [288], replicated, may hold values from 0 to 1, as said below
- cotangent: bfloat16 [288, 384, 384], P('lat', 'lon'), may hold values from -6 to 6
Outputs:
- out_fields: bfloat16 [288, 384, 384], P('lat', 'lon')
- field_grads: bfloat16 [288, 384, 384], P('lat', 'lon')
- table_grads: float32 [48, 6, 144, 23], P('lat', None, 'lon')
Inputs may be any that keep to these rules, and one draw needn't show every extreme that they name: `bias_table`: entries of order one; some heads and position pairs may carry large entries. `pad_rows`: every row is 1 except the last one or two rows of the grid, which are 0.
All inputs are finite; a program needn't handle non-finite values.
Results may differ from a plain program's by a relative error of at most 0.0095.
Values may be sent and summed in bfloat16 or wider, within the bound.
A program may use at most 64 MiB of HBM per device.

v0:
```python
import jax
import jax.numpy as jnp
from jax import lax
from jax.sharding import PartitionSpec as P

WIDTH = 192
HEADS = 6
HEAD_DIM = 32
LEVELS = 2
WIN_LAT = 6
WIN_LON = 12
TOKENS_WIN = 144
OFFSETS = 23
PAIRS = 144


epsilon_norm = 1e-05
masked_score = -1e30


def shifted(block, axis, distance):
    devices = range(lax.axis_size(axis))
    route = [((i - distance) % len(devices), i) for i in devices]
    return lax.ppermute(block, axis, route)


def sent_to_all(value, axis):
    copies = jnp.broadcast_to(value, (lax.axis_size(axis), *value.shape))
    return lax.all_to_all(copies, axis, split_axis=0, concat_axis=0, tiled=True)


def joined_along(parts, dim):
    shape = list(parts.shape[1:])
    shape[dim] *= parts.shape[0]
    return jnp.moveaxis(parts, 0, dim).reshape(shape)


def gathered_copies(value, axis, dim):
    parts = sent_to_all(value, axis)
    return joined_along(parts, dim)


def split_up(value, dim, length):
    before, after = (value.shape[:dim], value.shape[dim + 1 :])
    return jnp.moveaxis(value.reshape(*before, length, -1, *after), dim, 0)


def sent_and_summed(value, axis, dim):
    length = lax.axis_size(axis)
    parts = lax.all_to_all(split_up(value, dim, length), axis, 0, 0, tiled=True)
    return jnp.sum(parts, axis=0)


def norm_parts(inputs, norm_gain):
    wide_in = inputs.astype(jnp.float32)
    center = wide_in - jnp.mean(wide_in, axis=-1, keepdims=True)
    inverse_spread = lax.rsqrt(jnp.mean(center * center, axis=-1, keepdims=True) + epsilon_norm)
    normed = center * inverse_spread
    return (wide_in, normed, inverse_spread, (normed * norm_gain).astype(jnp.bfloat16))


def offset_selector():
    positions = jnp.arange(WIN_LON, dtype=jnp.int32)
    offsets_flat = (positions[:, None] - positions[None, :] + WIN_LON - 1).reshape(-1)
    return (jnp.arange(OFFSETS, dtype=jnp.int32)[:, None] == offsets_flat[None, :]).astype(
        jnp.float32
    )


def expand_bias(table_rows):
    count = table_rows.shape[0]
    zone = LEVELS * WIN_LAT
    spread = jnp.einsum(
        "rhpo,oq->rhpq", table_rows, offset_selector(), precision=lax.Precision.HIGHEST
    )
    spread = spread.reshape(count, HEADS, zone, zone, WIN_LON, WIN_LON).transpose(0, 1, 2, 4, 3, 5)
    return spread.reshape(count, HEADS, TOKENS_WIN, TOKENS_WIN)


def reduce_bias(grad_sums):
    count = grad_sums.shape[0]
    zone = LEVELS * WIN_LAT
    folded = grad_sums.reshape(count, HEADS, zone, WIN_LON, zone, WIN_LON).transpose(
        0, 1, 2, 4, 3, 5
    )
    folded = folded.reshape(count, HEADS, PAIRS, WIN_LON * WIN_LON)
    return jnp.einsum("rhpq,oq->rhpo", folded, offset_selector(), precision=lax.Precision.HIGHEST)


def to_windows(padded, window_rows, window_cols):
    shaped = padded.reshape(window_rows, WIN_LAT, window_cols, WIN_LON, LEVELS, WIDTH).transpose(
        0, 2, 4, 1, 3, 5
    )
    return shaped.reshape(window_rows, window_cols, TOKENS_WIN, WIDTH)


def from_windows(windowed):
    window_rows, window_cols = (windowed.shape[0], windowed.shape[1])
    shaped = windowed.reshape(window_rows, window_cols, LEVELS, WIN_LAT, WIN_LON, WIDTH).transpose(
        0, 3, 1, 4, 2, 5
    )
    return shaped.reshape(window_rows * WIN_LAT, window_cols * WIN_LON, LEVELS * WIDTH)


def attend_core(inputs, norm_gain, project_in, bias_block, allowed):
    wide_in, normed, inverse_spread, norm_fields = norm_parts(inputs, norm_gain)
    window_count, token_count = (inputs.shape[0], inputs.shape[1])
    projected = jnp.dot(norm_fields, project_in, preferred_element_type=jnp.float32).astype(
        jnp.bfloat16
    )
    heads_split = projected.reshape(window_count, token_count, 3, HEADS, HEAD_DIM)
    queries = heads_split[:, :, 0]
    key_rows = heads_split[:, :, 1]
    values = heads_split[:, :, 2]
    score_scale = HEAD_DIM ** (-0.5)
    scores = (
        jnp.einsum("bqhd,bkhd->bhqk", queries, key_rows, preferred_element_type=jnp.float32)
        * score_scale
        + bias_block[None]
    )
    scores = jnp.where(allowed[None, None], scores, masked_score)
    row_max = jnp.max(scores, axis=-1, keepdims=True)
    raised = jnp.exp(scores - row_max)
    weights_full = raised / jnp.sum(raised, axis=-1, keepdims=True)
    weights_low = weights_full.astype(jnp.bfloat16)
    mixed = jnp.einsum("bhqk,bkhd->bqhd", weights_low, values, preferred_element_type=jnp.float32)
    mixed = mixed.astype(jnp.bfloat16).reshape(window_count, token_count, WIDTH)
    return (
        wide_in,
        mixed,
        (normed, inverse_spread, queries, key_rows, values, weights_full, weights_low),
    )


def finish_output(wide_in, mixed, project_out):
    added = jnp.dot(mixed, project_out, preferred_element_type=jnp.float32)
    return (wide_in + added).astype(jnp.bfloat16)


def backprop(grads_out, norm_gain, project_in, project_out, saved):
    normed, inverse_spread, queries, key_rows, values, weights_full, weights_low = saved
    window_count, token_count = (grads_out.shape[0], grads_out.shape[1])
    score_scale = HEAD_DIM ** (-0.5)
    grad_mixed = jnp.einsum(
        "btj,cj->btc", grads_out, project_out, preferred_element_type=jnp.float32
    ).astype(jnp.bfloat16)
    grad_mixed = grad_mixed.reshape(window_count, token_count, HEADS, HEAD_DIM)
    grad_weights = jnp.einsum(
        "bqhd,bkhd->bhqk", grad_mixed, values, preferred_element_type=jnp.float32
    )
    grad_scores = weights_full * (
        grad_weights - jnp.sum(weights_full * grad_weights, axis=-1, keepdims=True)
    )
    grad_low = grad_scores.astype(jnp.bfloat16)
    grad_query = (
        jnp.einsum("bhqk,bkhd->bqhd", grad_low, key_rows, preferred_element_type=jnp.float32)
        * score_scale
    )
    grad_key = (
        jnp.einsum("bhqk,bqhd->bkhd", grad_low, queries, preferred_element_type=jnp.float32)
        * score_scale
    )
    grad_value = jnp.einsum(
        "bhqk,bqhd->bkhd", weights_low, grad_mixed, preferred_element_type=jnp.float32
    )
    grad_project = (
        jnp.stack([grad_query, grad_key, grad_value], axis=2)
        .reshape(window_count, token_count, 3 * WIDTH)
        .astype(jnp.bfloat16)
    )
    grad_norm = jnp.einsum(
        "btj,cj->btc", grad_project, project_in, preferred_element_type=jnp.float32
    )
    scaled_grad = grad_norm * norm_gain
    centered_grad = (
        scaled_grad
        - jnp.mean(scaled_grad, axis=-1, keepdims=True)
        - normed * jnp.mean(scaled_grad * normed, axis=-1, keepdims=True)
    )
    grad_input = (grads_out.astype(jnp.float32) + inverse_spread * centered_grad).astype(
        jnp.bfloat16
    )
    return (grad_input, grad_scores)


def window_mask(first_row, valid_rows, total_rows):
    token_band = jnp.arange(TOKENS_WIN, dtype=jnp.int32) // WIN_LON % WIN_LAT
    band_slots = jnp.arange(WIN_LAT, dtype=jnp.int32)
    token_rows = (first_row + token_band) % total_rows
    token_valid = jnp.sum(
        jnp.where(token_band[:, None] == band_slots[None, :], valid_rows[None, :], 0), axis=1
    )
    return (jnp.abs(token_rows[:, None] - token_rows[None, :]) < WIN_LAT) & (
        token_valid[None, :] == 1
    )


def valid_slice(pad_rows, row_start, length):
    total_rows = pad_rows.shape[0]
    doubled = jnp.concatenate([pad_rows, pad_rows])
    start = row_start % total_rows
    return lax.dynamic_slice_in_dim(doubled, start, length)


def run_windows(
    window_fields,
    window_grads,
    full_bias,
    row_start,
    valid_list,
    total_rows,
    norm_gain,
    project_in,
    project_out,
):
    window_rows = window_fields.shape[0]

    def one_row(window_row):
        first_row = row_start + WIN_LAT * window_row
        allowed = window_mask(first_row, valid_list, total_rows)
        wide_in, mixed, saved = attend_core(
            window_fields[window_row], norm_gain, project_in, full_bias[window_row], allowed
        )
        outputs = finish_output(wide_in, mixed, project_out)
        grad_input, grad_scores = backprop(
            window_grads[window_row], norm_gain, project_in, project_out, saved
        )
        return (outputs, grad_input, jnp.sum(grad_scores, axis=0))

    return lax.map(one_row, jnp.arange(window_rows, dtype=jnp.int32))


def per_device(fields, norm_gain, project_in, project_out, bias_table, pad_rows, cotangent):
    rows_here, cols_here, feature_width = fields.shape
    rim_rows = WIN_LAT // 2
    rim_cols = WIN_LON // 2
    band_index = lax.axis_index("lat")
    total_rows = rows_here * lax.axis_size("lat")
    table_here = rows_here // WIN_LAT
    stacked = jnp.concatenate([fields, cotangent], axis=2)
    below = shifted(stacked[:rim_rows], "lat", -1)
    taller = jnp.concatenate([stacked[rim_rows:], below], axis=0)
    beside = shifted(taller[:, :rim_cols], "lon", -1)
    moved = jnp.concatenate([taller[:, rim_cols:], beside], axis=1)
    table_rows = gathered_copies(bias_table, "lon", 2)
    full_bias = expand_bias(table_rows)
    window_cols = cols_here // WIN_LON
    row_start = band_index * rows_here + rim_rows
    valid_list = valid_slice(pad_rows, row_start, rows_here)
    window_fields = to_windows(moved[:, :, :feature_width], table_here, window_cols)
    window_grads = to_windows(moved[:, :, feature_width:], table_here, window_cols)
    out_windows, grad_windows, score_sums = run_windows(
        window_fields,
        window_grads,
        full_bias,
        row_start,
        valid_list,
        total_rows,
        norm_gain,
        project_in,
        project_out,
    )
    results = jnp.concatenate([from_windows(out_windows), from_windows(grad_windows)], axis=2)
    tail_cols = shifted(results[:, cols_here - rim_cols :], "lon", 1)
    wider = jnp.concatenate([tail_cols, results[:, : cols_here - rim_cols]], axis=1)
    tail_rows = shifted(wider[rows_here - rim_rows :], "lat", 1)
    placed = jnp.concatenate([tail_rows, wider[: rows_here - rim_rows]], axis=0)
    out_fields = placed[:, :, :feature_width]
    field_grads = placed[:, :, feature_width:]
    table_terms = reduce_bias(score_sums)
    table_grads = sent_and_summed(table_terms, "lon", 2)
    return (out_fields, field_grads, table_grads)


def solution(mesh):
    in_specs = (
        P("lat", "lon", None),
        P(),
        P(),
        P(),
        P("lat", None, "lon", None),
        P(),
        P("lat", "lon", None),
    )
    out_specs = (P("lat", "lon", None), P("lat", "lon", None), P("lat", None, "lon", None))
    return jax.shard_map(
        per_device, mesh=mesh, in_specs=in_specs, out_specs=out_specs, check_vma=False
    )
```

profile of v0, /device:TPU:6, one launch (start us, length us, event | category | flops | bytes accessed | tf_op | source)
XLA Modules:
  0.0 121.5 jit_solution(18144358416928707715)
XLA Ops:
  0.6 1.0 constant_dynamic-update-slice_fusion.1
  1.6 0.9 constant_dynamic-update-slice_fusion
  2.6 19.3 %collective-permute-start = (bf16[3,24,768]{2,1,0:T(8,128)(2,1)S(1)}, bf16[3,24,768]{2,1,0:T(8,128)(2,1)S(1)}, u32[]{:S(2)}, u32[]{:S(2)}) collective-permute-start(bf16[3,24,768]{2,1,0:T(8,128)(2,1)S(1)} %get-tuple-element.66), channel_id=1, source_target_pairs={{16,0},{32,16},{48,32},{64,48},{80,64},{96,80},{112,96},{128,112},... | collective-permute-start | bytes 331784 | tf_op jit(solution)/shard_map/ppermute | solution.py:24
  21.9 0.8 copy.276
  23.4 1.8 %reduce.3 = f32[16,6,9,23]{3,2,1,0:T(8,128)S(1)} reduce(f32[16,6,9,1,23]{4,3,2,1,0:T(1,128)S(1)} %broadcast_bitcast_fusion, f32[]{:T(128)} %broadcast.309), dimensions={3}, to_apply=%broadcast_bitcast_fusion.reduce_sub_computation | reduce | bytes 158980
  25.1 1.1 reshape.290
  26.2 5.1 %all-to-all-start = ((f32[16,1,1242]{2,1,0:T(1,128)}), f32[16,1,1242]{2,1,0:T(1,128)S(1)}, u32[]{:S(2)}, u32[]{:S(2)}) async-start(f32[16,1,1242]{2,1,0:T(1,128)} %reshape.290), calls=%async_computation | async-start | bytes 163840 | tf_op jit(solution)/shard_map/all_to_all | solution.py:29
  32.0 5.6 %collective-permute-start.1 = (bf16[6,6,768]{2,1,0:T(8,128)(2,1)S(1)}, bf16[6,6,768]{2,1,0:T(8,128)(2,1)S(1)}, u32[]{:S(2)}, u32[]{:S(2)}) collective-permute-start(bf16[6,6,768]{2,1,0:T(8,128)(2,1)S(1)} %pad_maximum_fusion.3), channel_id=1, source_target_pairs={{1,0},{2,1},{3,2},{4,3},{5,4},{6,5},{7,6},{8,7},{9,8},{10,9},{11,1... | collective-permute-start | bytes 165896 | tf_op jit(solution)/shard_map/ppermute | solution.py:24
  37.7 0.8 reduce.4
  39.2 4.9 %convolution_bitcast_fusion = f32[1,6,12,12,12,12]{4,5,2,1,3,0:T(8,128)} fusion(f32[6,12,12,23]{3,0,2,1:T(8,128)S(1)} %bitcast.134, pred[12,12,23,1,1]{2,1,0,3,4:T(8,128)(4,1)S(1)} %reshape.284), kind=kOutput, calls=%fused_computation.1 | convolution fusion | flops 34338816 | bytes 580464 | tf_op jit(solution)/shard_map/rhpo,oq->rhpq/dot_general | solution.py:73
  44.1 11.7 %copy.242 = f32[1,6,12,12,12,12]{3,2,5,4,1,0:T(8,128)} copy(f32[1,6,12,12,12,12]{4,5,2,1,3,0:T(8,128)} %convolution_bitcast_fusion) | data formatting | bytes 995328 | tf_op jit(solution)/shard_map/while/body/eval_jaxpr/add | solution.py:117
  55.8 5.7 %reshape.289 = f32[6,144,144]{1,2,0:T(8,128)} reshape(f32[1,6,12,12,12,12]{3,2,5,4,1,0:T(8,128)} %copy.242) | data formatting | bytes 995328 | tf_op jit(solution)/shard_map/while/body/eval_jaxpr/add | solution.py:117
  64.3 0.8 copy.218
  65.2 2.0 %fusion.41 = (f32[2,6,144]{2,1,0:T(8,128)S(1)}, f32[2,6,144,144]{2,3,1,0:T(8,128)S(1)}) fusion(f32[6,144,144]{1,2,0:T(8,128)} %reshape.289, pred[144,144]{0,1:T(8,128)(4,1)S(1)} %fusion.23, bf16[2,144,3,6,32]{1,4,3,2,0:T(8,128)(2,1)S(1)} %bitcast.140), kind=kOutput, calls=%fused_computation.96 | convolution fusion | flops 17169552 | bytes 1929984 | tf_op jit(solution)/shard_map/while/body/eval_jaxpr/sub | solution.py:123
  67.5 0.7 copy-done.5
  68.1 1.1 fusion.4
  70.2 0.6 copy-done.2
  72.2 0.6 fusion.38
  73.5 2.2 %collective-permute-start.2 = (bf16[6,6,768]{2,1,0:T(8,128)(2,1)S(1)}, bf16[6,6,768]{2,1,0:T(8,128)(2,1)S(1)}, u32[]{:S(2)}, u32[]{:S(2)}) collective-permute-start(bf16[6,6,768]{2,1,0:T(8,128)(2,1)S(1)} %slice.72), channel_id=1, source_target_pairs={{15,0},{0,1},{1,2},{2,3},{3,4},{4,5},{5,6},{6,7},{7,8},{8,9},{9,10... | collective-permute-start | bytes 165896 | tf_op jit(solution)/shard_map/ppermute | solution.py:24
  76.2 5.0 %reshape.278 = f32[1,6,12,12,12,12]{5,4,3,2,1,0:T(8,128)} reshape(f32[6,144,144]{2,1,0:T(8,128)S(1)} %copy.226) | data formatting | bytes 995328 | tf_op jit(solution)/shard_map/reshape | solution.py:83
  81.2 7.6 %copy.227 = f32[1,6,12,12,12,12]{5,4,1,3,2,0:T(8,128)} copy(f32[1,6,12,12,12,12]{5,3,4,2,1,0:T(8,128)} %bitcast.129) | data formatting | bytes 995328 | tf_op jit(solution)/shard_map/transpose | solution.py:83
  88.8 5.1 %reshape.279 = f32[6,16,9,144]{3,0,2,1:T(8,128)S(1)} reshape(f32[1,6,12,12,12,12]{5,4,1,3,2,0:T(8,128)} %copy.227) | data formatting | bytes 995328 | tf_op jit(solution)/shard_map/reshape.96
  93.9 0.8 convolution_bitcast_fusion.1
  95.1 1.8 %reduce.5 = f32[16,6,9,23]{3,2,1,0:T(8,128)S(1)} reduce(f32[16,6,9,1,23]{4,3,2,1,0:T(1,128)S(1)} %bitcast.138, f32[]{:T(128)} %broadcast.309), dimensions={3}, to_apply=%bitcast.127.reduce_sub_computation | reduce | bytes 158980
  96.9 1.1 reshape.292
  98.0 9.5 %all-to-all-start.1 = ((f32[16,1,1242]{2,1,0:T(1,128)}), f32[16,1,1242]{2,1,0:T(1,128)S(1)}, u32[]{:S(2)}, u32[]{:S(2)}) async-start(f32[16,1,1242]{2,1,0:T(1,128)} %reshape.292), calls=%async_computation.1 | async-start | bytes 163840 | tf_op jit(solution)/shard_map/all_to_all | solution.py:50
  107.5 1.9 %collective-permute-start.3 = (bf16[3,24,768]{2,1,0:T(8,128)(2,1)S(1)}, bf16[3,24,768]{2,1,0:T(8,128)(2,1)S(1)}, u32[]{:S(2)}, u32[]{:S(2)}) collective-permute-start(bf16[3,24,768]{2,1,0:T(8,128)(2,1)S(1)} %fusion.25), channel_id=1, source_target_pairs={{752,0},{0,16},{16,32},{32,48},{48,64},{64,80},{80,96},{96,112},{1... | collective-permute-start | bytes 331784 | tf_op jit(solution)/shard_map/ppermute | solution.py:24
  109.4 4.2 %all-to-all-done.1 = f32[16,1,1242]{2,1,0:T(1,128)S(1)} async-done(((f32[16,1,1242]{2,1,0:T(1,128)}), f32[16,1,1242]{2,1,0:T(1,128)S(1)}, u32[]{:S(2)}, u32[]{:S(2)}) %all-to-all-start.1) | async-done | bytes 79520 | tf_op jit(solution)/shard_map/all_to_all | solution.py:50
  113.7 0.8 reduce.6
  115.4 0.6 copy.232
  116.1 4.7 %collective-permute-done.3 = bf16[3,24,768]{2,1,0:T(8,128)(2,1)S(1)} collective-permute-done((bf16[3,24,768]{2,1,0:T(8,128)(2,1)S(1)}, bf16[3,24,768]{2,1,0:T(8,128)(2,1)S(1)}, u32[]{:S(2)}, u32[]{:S(2)}) %collective-permute-start.3) | collective-permute-done | bytes 110624 | tf_op jit(solution)/shard_map/ppermute | solution.py:24
  120.8 0.7 fusion.39
  (77 shorter events, 9.9 us)
Async XLA Ops:
  0.6 62.6 %copy-start = (bf16[192,576]{1,0:T(8,128)(2,1)S(1)}, bf16[192,576]{1,0:T(8,128)(2,1)}, u32[]{:S(2)}) copy-start(bf16[192,576]{1,0:T(8,128)(2,1)} %param.9) | copy-start | bytes 663556
  1.6 29.9 %copy-start.7 = (s32[288]{0:T(512)S(1)}, s32[288]{0:T(512)}, u32[]{:S(2)}) copy-start(s32[288]{0:T(512)} %param.12) | copy-start | bytes 3460
  2.6 29.4 %collective-permute-start = (bf16[3,24,768]{2,1,0:T(8,128)(2,1)S(1)}, bf16[3,24,768]{2,1,0:T(8,128)(2,1)S(1)}, u32[]{:S(2)}, u32[]{:S(2)}) collective-permute-start(bf16[3,24,768]{2,1,0:T(8,128)(2,1)S(1)} %get-tuple-element.66), channel_id=1, source_target_pairs={{16,0},{32,16},{48,32},{64,48},{80,64},{96,80},{112,96},{128,112},... | collective-permute-start | bytes 331784 | tf_op jit(solution)/shard_map/ppermute | solution.py:24
  26.2 11.6 %all-to-all-start = ((f32[16,1,1242]{2,1,0:T(1,128)}), f32[16,1,1242]{2,1,0:T(1,128)S(1)}, u32[]{:S(2)}, u32[]{:S(2)}) async-start(f32[16,1,1242]{2,1,0:T(1,128)} %reshape.290), calls=%async_computation | async-start | bytes 163840 | tf_op jit(solution)/shard_map/all_to_all | solution.py:29
  32.0 29.5 %collective-permute-start.1 = (bf16[6,6,768]{2,1,0:T(8,128)(2,1)S(1)}, bf16[6,6,768]{2,1,0:T(8,128)(2,1)S(1)}, u32[]{:S(2)}, u32[]{:S(2)}) collective-permute-start(bf16[6,6,768]{2,1,0:T(8,128)(2,1)S(1)} %pad_maximum_fusion.3), channel_id=1, source_target_pairs={{1,0},{2,1},{3,2},{4,3},{5,4},{6,5},{7,6},{8,7},{9,8},{10,9},{11,1... | collective-permute-start | bytes 165896 | tf_op jit(solution)/shard_map/ppermute | solution.py:24
  61.5 1.7 %copy-start.6 = (f32[192]{0:T(256)S(1)}, f32[192]{0:T(256)}, u32[]{:S(2)}) copy-start(f32[192]{0:T(256)} %param.8) | copy-start | bytes 2308
  62.2 1.9 %copy-start.3 = (bf16[192,192]{1,0:T(8,128)(2,1)S(1)}, bf16[192,192]{1,0:T(8,128)(2,1)}, u32[]{:S(2)}) copy-start(bf16[192,192]{1,0:T(8,128)(2,1)} %param.10) | copy-start | bytes 221188
  63.9 5.3 %copy-start.1 = (bf16[2,144,576]{1,2,0:T(8,128)(2,1)}, bf16[2,144,576]{1,2,0:T(8,128)(2,1)S(1)}, u32[]{:S(2)}) copy-start(bf16[2,144,576]{1,2,0:T(8,128)(2,1)S(1)} %copy.200) | copy-start | bytes 995332
  67.2 0.9 copy-start.5
  69.7 1.1 copy-start.2
  71.1 0.9 copy-start.4
  73.5 33.9 %collective-permute-start.2 = (bf16[6,6,768]{2,1,0:T(8,128)(2,1)S(1)}, bf16[6,6,768]{2,1,0:T(8,128)(2,1)S(1)}, u32[]{:S(2)}, u32[]{:S(2)}) collective-permute-start(bf16[6,6,768]{2,1,0:T(8,128)(2,1)S(1)} %slice.72), channel_id=1, source_target_pairs={{15,0},{0,1},{1,2},{2,3},{3,4},{4,5},{5,6},{6,7},{7,8},{8,9},{9,10... | collective-permute-start | bytes 165896 | tf_op jit(solution)/shard_map/ppermute | solution.py:24
  98.0 15.7 %all-to-all-start.1 = ((f32[16,1,1242]{2,1,0:T(1,128)}), f32[16,1,1242]{2,1,0:T(1,128)S(1)}, u32[]{:S(2)}, u32[]{:S(2)}) async-start(f32[16,1,1242]{2,1,0:T(1,128)} %reshape.292), calls=%async_computation.1 | async-start | bytes 163840 | tf_op jit(solution)/shard_map/all_to_all | solution.py:50
  107.5 13.3 %collective-permute-start.3 = (bf16[3,24,768]{2,1,0:T(8,128)(2,1)S(1)}, bf16[3,24,768]{2,1,0:T(8,128)(2,1)S(1)}, u32[]{:S(2)}, u32[]{:S(2)}) collective-permute-start(bf16[3,24,768]{2,1,0:T(8,128)(2,1)S(1)} %fusion.25), channel_id=1, source_target_pairs={{752,0},{0,16},{16,32},{32,48},{48,64},{64,80},{80,96},{96,112},{1... | collective-permute-start | bytes 331784 | tf_op jit(solution)/shard_map/ppermute | solution.py:24
where the time goes:
time: 123 us; the launch traced here: 122 us
  local copies, waits for them, and re-layouts  48.5 us (39%)
  starting transfers between devices  43.7 us (36%)
  matrix products  11.5 us (9%)
  waiting for transfers between devices  8.99 us (7%)
  other arithmetic  7.7 us (6%)
    ppermute x4, starting transfers between devices, shifted(): return lax.ppermute(block, axis, route)  29.1 us
    add x2, local copies, waits for them, and re-layouts, attend_core(): jnp.einsum('bqhd,bkhd->bhqk', queries, key_rows, preferred_element_type=j...  17.4 us
    all_to_all x1, starting transfers between devices, sent_and_summed(): parts = lax.all_to_all(split_up(value, dim, length), axis, 0, 0, tiled=True)  9.51 us
    transpose x1, local copies, waits for them, and re-layouts, reduce_bias(): grad_sums.reshape(count, HEADS, zone, WIN_LON, zone, WIN_LON)  7.62 us
    unnamed x25, local copies, waits for them, and re-layouts  6.84 us
    another operation x2, local copies, waits for them, and re-layouts  5.84 us
    all_to_all x1, starting transfers between devices, sent_to_all(): return lax.all_to_all(copies, axis, split_axis=0, concat_axis=0, tiled=True)  5.14 us
    reshape x1, local copies, waits for them, and re-layouts, reduce_bias(): grad_sums.reshape(count, HEADS, zone, WIN_LON, zone, WIN_LON)  4.98 us
  transfers between devices with their start and end apart: 6, of which 2 were waited for; matrix products, arithmetic and copies ran while one was open for 44% of the time, Pallas kernels for 0%

commit v1 on v0

v1 whole, which is shorter than its diff:
```python
import functools

import jax
import jax.numpy as jnp
from jax import lax
from jax.experimental import pallas as pl
from jax.experimental.pallas import tpu as pltpu
from jax.sharding import PartitionSpec as P

WIDTH = 192
HEADS = 6
HEAD_DIM = 32
LEVELS = 2
WIN_LAT = 6
WIN_LON = 12
ZONE = LEVELS * WIN_LAT
CELLS = WIN_LAT * WIN_LON
TOKENS = LEVELS * CELLS
OFFSETS = 23
SLOT = 24
PAIRS = ZONE * ZONE
RIM_R = WIN_LAT // 2
RIM_C = WIN_LON // 2
WINDOWS = 2
COLS = WINDOWS * WIN_LON
FEATS = LEVELS * WIDTH
BAND = 384
DOWN = 56
SIDE = 24
SCALE = HEAD_DIM**-0.5
EPS = 1e-05
MASKED = -1e30
MESH = pl.DeviceIdType.MESH
F32 = jnp.float32
BF16 = jnp.bfloat16


def dot_nn(a, b):
    return lax.dot_general(a, b, (((1,), (0,)), ((), ())), preferred_element_type=F32)


def dot_nt(a, b):
    return lax.dot_general(a, b, (((1,), (1,)), ((), ())), preferred_element_type=F32)


def dot_tn(a, b):
    return lax.dot_general(a, b, (((0,), (0,)), ((), ())), preferred_element_type=F32)


def kernel(
    lat_size,
    lon_size,
    pairs_here,
    fields_hbm,
    gain_hbm,
    win_hbm,
    wout_hbm,
    bias_hbm,
    pad_hbm,
    cot_hbm,
    out_ref,
    grads_ref,
    table_ref,
    f_in,
    c_in,
    w_in,
    wo_in,
    bias_in,
    gain_ref,
    pad_ref,
    raw,
    xw,
    cw,
    tmp,
    send_down,
    send_side,
    recv_down,
    recv_side,
    bias_msg,
    bias_recv,
    spread,
    bias_flat,
    bias_full,
    w_t,
    xtok,
    ctok,
    xhat,
    spread_inv,
    proj_t,
    k_nat,
    v_nat,
    gmix_t,
    mixed_t,
    gproj_t,
    gflat,
    cells,
    table_msg,
    table_recv,
    in_sem,
    halo_send,
    halo_recv,
    bias_send,
    bias_rsem,
    table_send,
    table_rsem,
):
    lat = lax.axis_index("lat")
    lon = lax.axis_index("lon")
    up = lax.rem(lat + lat_size - 1, lat_size)
    dn = lax.rem(lat + 1, lat_size)
    lf = lax.rem(lon + lon_size - 1, lon_size)
    rt = lax.rem(lon + 1, lon_size)

    barrier = pltpu.get_barrier_semaphore()
    for dev in ((up, lon), (up, lf), (dn, lon), (dn, rt)):
        pl.semaphore_signal(barrier, inc=1, device_id=dev, device_id_type=MESH)

    def greet(s, carry):
        peer = lax.rem(lon + s, lon_size)
        pl.semaphore_signal(barrier, inc=1, device_id=(lat, peer), device_id_type=MESH)
        return carry

    lax.fori_loop(1, lon_size, greet, 0)

    loads = [
        pltpu.make_async_copy(src, dst, in_sem.at[n])
        for n, (src, dst) in enumerate(
            (
                (fields_hbm, f_in),
                (cot_hbm, c_in),
                (bias_hbm, bias_in),
                (win_hbm, w_in),
                (wout_hbm, wo_in),
                (gain_hbm, gain_ref),
                (pad_hbm, pad_ref),
            )
        )
    ]
    for load in loads:
        load.start()

    def halo_copy(kind, piece):
        inward = kind < 2
        row_dev, col_dev = (up, lf) if inward else (dn, rt)
        dev = ((row_dev, lon), (lat, col_dev), (row_dev, col_dev))[piece]
        if piece == 0:
            src, dst = send_down.at[kind], recv_down.at[kind]
        else:
            src, dst = send_side.at[kind, piece - 1], recv_side.at[kind, piece - 1]
        return pltpu.make_async_remote_copy(
            src_ref=src,
            dst_ref=dst,
            send_sem=halo_send.at[kind, piece],
            recv_sem=halo_recv.at[kind, piece],
            device_id=dev,
            device_id_type=MESH,
        )

    def pack_in(src, kind, windows):
        for r in range(WIN_LAT):
            raw[r * COLS : (r + 1) * COLS, :] = src[r].astype(F32)
        for r in range(RIM_R):
            base = r * COLS
            tmp[r * 12 : r * 12 + 12, :] = raw[base + 6 : base + 18, :]
            tmp[36 + r * 6 : 42 + r * 6, :] = raw[base + 18 : base + 24, :]
            tmp[88 + r * 6 : 94 + r * 6, :] = raw[base : base + 6, :]
            below = (r + RIM_R) * COLS
            tmp[64 + r * 6 : 70 + r * 6, :] = raw[below : below + 6, :]
            windows[r * 12 : r * 12 + 12, :] = raw[below + 6 : below + 18, :]
            windows[CELLS + r * 12 : CELLS + r * 12 + 6, :] = raw[below + 18 : below + 24, :]
        send_down[kind] = tmp[0:DOWN, :].astype(BF16)
        send_side[kind, 0] = tmp[64 : 64 + SIDE, :].astype(BF16)
        send_side[kind, 1] = tmp[88 : 88 + SIDE, :].astype(BF16)

    def unpack_in(kind, windows):
        tmp[0:DOWN, :] = recv_down[kind].astype(F32)
        tmp[64 : 64 + SIDE, :] = recv_side[kind, 0].astype(F32)
        tmp[88 : 88 + SIDE, :] = recv_side[kind, 1].astype(F32)
        windows[36:72, :] = tmp[0:36, :]
        for r in range(RIM_R):
            top = CELLS + r * 12
            low = CELLS + (r + RIM_R) * 12
            windows[low : low + 6, :] = tmp[36 + r * 6 : 42 + r * 6, :]
            windows[top + 6 : top + 12, :] = tmp[64 + r * 6 : 70 + r * 6, :]
            windows[low + 6 : low + 12, :] = tmp[88 + r * 6 : 94 + r * 6, :]

    tmp[...] = jnp.zeros_like(tmp)
    loads[0].wait()
    pack_in(f_in, 0, xw)
    loads[2].wait()
    bias_msg[...] = jnp.zeros_like(bias_msg)
    for r in range(pairs_here):
        for h in range(HEADS):
            bias_msg[h : h + 1, r * SLOT : r * SLOT + OFFSETS] = bias_in[h, r]
    bias_recv[lon] = bias_msg[...]
    loads[1].wait()
    pack_in(c_in, 1, cw)

    pl.semaphore_wait(barrier, lon_size + 3)

    def bias_copy(s):
        peer = lax.rem(lon + s, lon_size)
        return pltpu.make_async_remote_copy(
            src_ref=bias_msg,
            dst_ref=bias_recv.at[lon],
            send_sem=bias_send.at[s],
            recv_sem=bias_rsem.at[lon],
            device_id=(lat, peer),
            device_id_type=MESH,
        )

    def bias_arrival(s):
        source = lax.rem(lon + s, lon_size)
        return pltpu.make_async_remote_copy(
            src_ref=bias_msg,
            dst_ref=bias_recv.at[source],
            send_sem=bias_send.at[s],
            recv_sem=bias_rsem.at[source],
            device_id=(lat, source),
            device_id_type=MESH,
        )

    for piece in (0, 2, 1):
        halo_copy(0, piece).start()

    def send_bias(s, carry):
        bias_copy(s).start()
        return carry

    lax.fori_loop(1, lon_size, send_bias, 0)
    for piece in (0, 2, 1):
        halo_copy(1, piece).start()

    gflat[...] = jnp.zeros_like(gflat)
    table_msg[...] = jnp.zeros_like(table_msg)
    spread[...] = jnp.zeros_like(spread)
    lane = lax.broadcasted_iota(jnp.int32, (BAND, TOKENS), 0)
    query = lax.broadcasted_iota(jnp.int32, (BAND, TOKENS), 1)
    picked = (query // WIN_LON) * SLOT + query % WIN_LON + WIN_LON - 1
    selector = (lane == picked).astype(F32).astype(BF16)
    loads[3].wait()
    loads[4].wait()
    loads[5].wait()
    loads[6].wait()
    w_t[...] = w_in[...].astype(F32).T.astype(BF16)

    total_rows = lat_size * WIN_LAT
    first_row = lat * WIN_LAT + RIM_R
    key_band = (lax.broadcasted_iota(jnp.int32, (TOKENS, TOKENS), 0) // WIN_LON) % WIN_LAT
    query_band = (lax.broadcasted_iota(jnp.int32, (TOKENS, TOKENS), 1) // WIN_LON) % WIN_LAT
    key_row = lax.rem(first_row + key_band, total_rows)
    query_row = lax.rem(first_row + query_band, total_rows)
    real = jnp.zeros((TOKENS, TOKENS), jnp.int32)
    for a in range(WIN_LAT):
        real = jnp.where(key_band == a, pad_ref[lax.rem(first_row + a, total_rows)], real)
    allowed = (jnp.abs(query_row - key_row) < WIN_LAT) & (real == 1)

    def wait_bias(s, carry):
        bias_arrival(s).wait_recv()
        return carry

    lax.fori_loop(1, lon_size, wait_bias, 0)
    for p in range(PAIRS):
        owner, r = p // pairs_here, p % pairs_here
        zq, zt = p // ZONE, p % ZONE
        spread[zt * 8 : zt * 8 + 8, zq * SLOT : (zq + 1) * SLOT] = bias_recv[
            owner, :, r * SLOT : (r + 1) * SLOT
        ]
    for b in range(WIN_LON):
        table = spread[...]
        if b:
            table = pltpu.roll(table, b, 1)
        high = table.astype(BF16)
        rest = table - high.astype(F32)
        middle = rest.astype(BF16)
        low = (rest - middle.astype(F32)).astype(BF16)
        wide = dot_nn(high, selector) + (dot_nn(middle, selector) + dot_nn(low, selector))
        for zt in range(ZONE):
            row = (zt * WIN_LON + b) * 8
            bias_flat[0, row : row + 8, :] = wide[zt * 8 : zt * 8 + 8, 0:128]
            bias_flat[1, row : row + 8, 0 : TOKENS - 128] = wide[zt * 8 : zt * 8 + 8, 128:TOKENS]
    for h in range(HEADS):
        left = bias_flat[0, pl.ds(h, TOKENS, stride=8), :]
        right = bias_flat[1, pl.ds(h, TOKENS, stride=8), :]
        whole = jnp.concatenate([left, right[:, 0 : TOKENS - 128]], axis=1)
        bias_full[h] = jnp.where(allowed, whole, MASKED)

    gain = gain_ref[...]
    for piece in range(3):
        halo_copy(0, piece).wait_recv()
    unpack_in(0, xw)
    for w in range(WINDOWS):
        block = xw[w * CELLS : (w + 1) * CELLS, :]
        x = jnp.concatenate([block[:, :WIDTH], block[:, WIDTH:]], axis=0)
        xtok[w] = x
        center = x - jnp.mean(x, axis=1, keepdims=True)
        inverse = lax.rsqrt(jnp.mean(center * center, axis=1, keepdims=True) + EPS)
        normed = center * inverse
        xhat[w] = normed
        spread_inv[w] = inverse
        x_n = (normed * gain).astype(BF16)
        proj_t[w] = dot_nt(w_t[...], x_n).astype(BF16)
        kv = dot_nn(x_n, w_in[:, WIDTH:]).astype(BF16)
        for h in range(HEADS):
            k_nat[w, h] = kv[:, h * HEAD_DIM : (h + 1) * HEAD_DIM]
            v_nat[w, h] = kv[:, WIDTH + h * HEAD_DIM : WIDTH + (h + 1) * HEAD_DIM]
    for piece in range(3):
        halo_copy(1, piece).wait_recv()
    unpack_in(1, cw)
    for w in range(WINDOWS):
        block = cw[w * CELLS : (w + 1) * CELLS, :]
        c = jnp.concatenate([block[:, :WIDTH], block[:, WIDTH:]], axis=0)
        ctok[w] = c
        gmix_t[w] = dot_nt(wo_in[...], c.astype(BF16)).astype(BF16)

    def one_head(h, carry):
        at_q = pl.ds(pl.multiple_of(h * HEAD_DIM, HEAD_DIM), HEAD_DIM)
        at_k = pl.ds(pl.multiple_of(WIDTH + h * HEAD_DIM, HEAD_DIM), HEAD_DIM)
        at_v = pl.ds(pl.multiple_of(2 * WIDTH + h * HEAD_DIM, HEAD_DIM), HEAD_DIM)
        bias = bias_full[h]
        summed = None
        for w in range(WINDOWS):
            q_t = proj_t[w, at_q, :]
            g_t = gmix_t[w, at_q, :]
            scores = dot_nn(k_nat[w, h], q_t) * SCALE + bias
            raised = jnp.exp(scores - jnp.max(scores, axis=0, keepdims=True))
            weights = raised * (1.0 / jnp.sum(raised, axis=0, keepdims=True))
            weights_low = weights.astype(BF16)
            mixed_t[w, at_q, :] = dot_nn(proj_t[w, at_v, :], weights_low).astype(BF16)
            grad_w = dot_nn(v_nat[w, h], g_t)
            grad_s = weights * (grad_w - jnp.sum(weights * grad_w, axis=0, keepdims=True))
            grad_low = grad_s.astype(BF16)
            gproj_t[w, at_q, :] = (dot_nn(proj_t[w, at_k, :], grad_low) * SCALE).astype(BF16)
            gproj_t[w, at_k, :] = (dot_nt(q_t, grad_low) * SCALE).astype(BF16)
            gproj_t[w, at_v, :] = dot_nt(g_t, weights_low).astype(BF16)
            summed = grad_s if summed is None else summed + grad_s
        gflat[0, pl.ds(h, TOKENS, stride=8), :] = summed[:, 0:128]
        gflat[1, pl.ds(h, TOKENS, stride=8), 0 : TOKENS - 128] = summed[:, 128:TOKENS]
        return carry

    for h in range(HEADS):
        one_head(h, 0)

    def give_back(kind, tokens):
        for w in range(WINDOWS):
            cells[w * CELLS : (w + 1) * CELLS, 0:WIDTH] = tokens[w][0:CELLS]
            cells[w * CELLS : (w + 1) * CELLS, WIDTH:] = tokens[w][CELLS:]
        tmp[0:36, :] = cells[36:72, :]
        for r in range(RIM_R):
            top = CELLS + r * 12
            low = CELLS + (r + RIM_R) * 12
            tmp[36 + r * 6 : 42 + r * 6, :] = cells[low : low + 6, :]
            tmp[64 + r * 6 : 70 + r * 6, :] = cells[top + 6 : top + 12, :]
            tmp[88 + r * 6 : 94 + r * 6, :] = cells[low + 6 : low + 12, :]
        send_down[kind] = tmp[0:DOWN, :].astype(BF16)
        send_side[kind, 0] = tmp[64 : 64 + SIDE, :].astype(BF16)
        send_side[kind, 1] = tmp[88 : 88 + SIDE, :].astype(BF16)
        for piece in (0, 2, 1):
            halo_copy(kind, piece).start()
        own = raw if kind == 2 else xw
        for r in range(RIM_R):
            below = (r + RIM_R) * COLS
            own[below + 6 : below + 18, :] = cells[r * 12 : r * 12 + 12, :]
            own[below + 18 : below + 24, :] = cells[CELLS + r * 12 : CELLS + r * 12 + 6, :]

    def take_back(kind, dst):
        own = raw if kind == 2 else xw
        for piece in range(3):
            halo_copy(kind, piece).wait_recv()
        tmp[0:DOWN, :] = recv_down[kind].astype(F32)
        tmp[64 : 64 + SIDE, :] = recv_side[kind, 0].astype(F32)
        tmp[88 : 88 + SIDE, :] = recv_side[kind, 1].astype(F32)
        for r in range(RIM_R):
            base = r * COLS
            below = (r + RIM_R) * COLS
            own[base + 6 : base + 18, :] = tmp[r * 12 : r * 12 + 12, :]
            own[base + 18 : base + 24, :] = tmp[36 + r * 6 : 42 + r * 6, :]
            own[base : base + 6, :] = tmp[88 + r * 6 : 94 + r * 6, :]
            own[below : below + 6, :] = tmp[64 + r * 6 : 70 + r * 6, :]
        for r in range(WIN_LAT):
            dst[r] = own[r * COLS : (r + 1) * COLS, :].astype(BF16)

    give_back(2, [xtok[w] + dot_tn(mixed_t[w], wo_in[...]) for w in range(WINDOWS)])

    grads = []
    for w in range(WINDOWS):
        scaled = dot_tn(gproj_t[w], w_t[...]) * gain
        normed = xhat[w]
        centered = (
            scaled
            - jnp.mean(scaled, axis=1, keepdims=True)
            - normed * jnp.mean(scaled * normed, axis=1, keepdims=True)
        )
        grads.append(ctok[w] + spread_inv[w] * centered)
    give_back(3, grads)

    total = jnp.zeros((ZONE * 8, BAND), F32)
    for b in range(WIN_LON):
        picked_rows = []
        for zt in range(ZONE):
            row = (zt * WIN_LON + b) * 8
            picked_rows.append(
                jnp.concatenate(
                    [
                        gflat[0, row : row + 8, :],
                        gflat[1, row : row + 8, 0 : TOKENS - 128],
                    ],
                    axis=1,
                )
            )
        part = jnp.concatenate(picked_rows, axis=0)
        high = part.astype(BF16)
        low = (part - high.astype(F32)).astype(BF16)
        placed = dot_nt(high, selector) + dot_nt(low, selector)
        if b:
            placed = pltpu.roll(placed, BAND - b, 1)
        total = total + placed
    spread[...] = total
    for p in range(PAIRS):
        owner, r = p // pairs_here, p % pairs_here
        zq, zt = p // ZONE, p % ZONE
        table_msg[owner, :, r * SLOT : (r + 1) * SLOT] = spread[
            zt * 8 : zt * 8 + 8, zq * SLOT : (zq + 1) * SLOT
        ]

    def table_copy(s):
        peer = lax.rem(lon + s, lon_size)
        return pltpu.make_async_remote_copy(
            src_ref=table_msg.at[peer],
            dst_ref=table_recv.at[lon],
            send_sem=table_send.at[s],
            recv_sem=table_rsem.at[lon],
            device_id=(lat, peer),
            device_id_type=MESH,
        )

    def table_arrival(s):
        source = lax.rem(lon + s, lon_size)
        return pltpu.make_async_remote_copy(
            src_ref=table_msg.at[source],
            dst_ref=table_recv.at[source],
            send_sem=table_send.at[s],
            recv_sem=table_rsem.at[source],
            device_id=(lat, source),
            device_id_type=MESH,
        )

    def send_table(s, carry):
        table_copy(s).start()
        return carry

    lax.fori_loop(1, lon_size, send_table, 0)
    table_recv[lon] = table_msg[lon]

    take_back(2, out_ref)
    take_back(3, grads_ref)

    def wait_table(s, carry):
        table_arrival(s).wait_recv()
        return carry

    lax.fori_loop(1, lon_size, wait_table, 0)
    added = table_recv[0]
    for j in range(1, lon_size):
        added = added + table_recv[j]
    bias_msg_out = added
    for r in range(pairs_here):
        piece = bias_msg_out[:, r * SLOT : r * SLOT + OFFSETS]
        for h in range(HEADS):
            table_ref[h, r] = piece[h : h + 1, :]

    for kind in range(4):
        for piece in range(3):
            halo_copy(kind, piece).wait_send()

    def drain(s, carry):
        bias_copy(s).wait_send()
        table_copy(s).wait_send()
        return carry

    lax.fori_loop(1, lon_size, drain, 0)


def solution(mesh):
    lat_size, lon_size = mesh.shape["lat"], mesh.shape["lon"]
    pairs_here = PAIRS // lon_size
    lanes = -(-pairs_here * SLOT // 128) * 128

    def per_device(fields, norm_gain, project_in, project_out, bias_table, pad_rows, cotangent):
        hbm_spec = pl.BlockSpec(memory_space=pltpu.HBM)
        vmem_spec = pl.BlockSpec(memory_space=pltpu.VMEM)
        out_fields, field_grads, table_grads = pl.pallas_call(
            functools.partial(kernel, lat_size, lon_size, pairs_here),
            out_shape=(
                jax.ShapeDtypeStruct(fields.shape, BF16),
                jax.ShapeDtypeStruct(fields.shape, BF16),
                jax.ShapeDtypeStruct((HEADS, pairs_here, 1, OFFSETS), F32),
            ),
            in_specs=[hbm_spec] * 7,
            out_specs=(vmem_spec, vmem_spec, vmem_spec),
            scratch_shapes=[
                pltpu.VMEM(fields.shape, BF16),
                pltpu.VMEM(fields.shape, BF16),
                pltpu.VMEM(project_in.shape, BF16),
                pltpu.VMEM(project_out.shape, BF16),
                pltpu.VMEM((HEADS, pairs_here, 1, OFFSETS), F32),
                pltpu.VMEM((1, WIDTH), F32),
                pltpu.SMEM(pad_rows.shape, jnp.int32),
                pltpu.VMEM((WIN_LAT * COLS, FEATS), F32),
                pltpu.VMEM((WINDOWS * CELLS, FEATS), F32),
                pltpu.VMEM((WINDOWS * CELLS, FEATS), F32),
                pltpu.VMEM((112, FEATS), F32),
                pltpu.VMEM((4, DOWN, FEATS), BF16),
                pltpu.VMEM((4, 2, SIDE, FEATS), BF16),
                pltpu.VMEM((4, DOWN, FEATS), BF16),
                pltpu.VMEM((4, 2, SIDE, FEATS), BF16),
                pltpu.VMEM((8, lanes), F32),
                pltpu.VMEM((lon_size, 8, lanes), F32),
                pltpu.VMEM((ZONE * 8, BAND), F32),
                pltpu.VMEM((2, TOKENS * 8, 128), F32),
                pltpu.VMEM((HEADS, TOKENS, TOKENS), F32),
                pltpu.VMEM((3 * WIDTH, WIDTH), BF16),
                pltpu.VMEM((WINDOWS, TOKENS, WIDTH), F32),
                pltpu.VMEM((WINDOWS, TOKENS, WIDTH), F32),
                pltpu.VMEM((WINDOWS, TOKENS, WIDTH), F32),
                pltpu.VMEM((WINDOWS, TOKENS, 1), F32),
                pltpu.VMEM((WINDOWS, 3 * WIDTH, TOKENS), BF16),
                pltpu.VMEM((WINDOWS, HEADS, TOKENS, HEAD_DIM), BF16),
                pltpu.VMEM((WINDOWS, HEADS, TOKENS, HEAD_DIM), BF16),
                pltpu.VMEM((WINDOWS, WIDTH, TOKENS), BF16),
                pltpu.VMEM((WINDOWS, WIDTH, TOKENS), BF16),
                pltpu.VMEM((WINDOWS, 3 * WIDTH, TOKENS), BF16),
                pltpu.VMEM((2, TOKENS * 8, 128), F32),
                pltpu.VMEM((WINDOWS * CELLS, FEATS), F32),
                pltpu.VMEM((lon_size, 8, lanes), F32),
                pltpu.VMEM((lon_size, 8, lanes), F32),
                pltpu.SemaphoreType.DMA((7,)),
                pltpu.SemaphoreType.DMA((4, 3)),
                pltpu.SemaphoreType.DMA((4, 3)),
                pltpu.SemaphoreType.DMA((lon_size,)),
                pltpu.SemaphoreType.DMA((lon_size,)),
                pltpu.SemaphoreType.DMA((lon_size,)),
                pltpu.SemaphoreType.DMA((lon_size,)),
            ],
            compiler_params=pltpu.CompilerParams(
                collective_id=0, has_side_effects=True, vmem_limit_bytes=48 << 20
            ),
        )(
            *(
                pltpu.with_memory_space_constraint(x, pltpu.HBM)
                for x in (
                    fields,
                    norm_gain.reshape(1, WIDTH),
                    project_in,
                    project_out,
                    bias_table.reshape(HEADS, pairs_here, 1, OFFSETS),
                    pad_rows,
                    cotangent,
                )
            )
        )
        return out_fields, field_grads, table_grads.reshape(bias_table.shape)

    in_specs = (
        P("lat", "lon", None),
        P(),
        P(),
        P(),
        P("lat", None, "lon", None),
        P(),
        P("lat", "lon", None),
    )
    out_specs = (P("lat", "lon", None), P("lat", "lon", None), P("lat", None, "lon", None))
    return jax.shard_map(
        per_device, mesh=mesh, in_specs=in_specs, out_specs=out_specs, check_vma=False
    )
```

time: 123 us -> 45.3 us (0.37); the launches traced: 122 us -> 45.2 us
  local copies, waits for them, and re-layouts: 48.5 us -> 1.9 us
  starting transfers between devices: 43.7 us -> 0 us
  Pallas kernels: 0 us -> 42.6 us
  matrix products: 11.5 us -> 0 us
  waiting for transfers between devices: 8.99 us -> 0 us
  other arithmetic: 7.7 us -> 0 us
    pallas_call x0 -> x1, Pallas kernels: none -> 42.6 us  [per_device(): pl.pallas_call(functools.partial(kernel, lat_size, lon_size, pairs_here),...]
    ppermute x4 -> x0, starting transfers between devices: 29.1 us -> none  [shifted(): return lax.ppermute(block, axis, route)]
    add x2 -> x0, local copies, waits for them, and re-layouts: 17.4 us -> none  [attend_core(): jnp.einsum('bqhd,bkhd->bhqk', queries, key_rows, preferred_element_type=j...]
    all_to_all x2 -> x0, starting transfers between devices: 14.6 us -> none  [the longest x1 9.51 us: sent_and_summed(): parts = lax.all_to_all(split_up(value, dim, length), axis, 0, 0, tiled=True)]
    dot_general x11 -> x0, matrix products: 9.51 us -> none  [the longest x1 4.91 us: expand_bias(): jnp.einsum('rhpo,oq->rhpq', table_rows, offset_selector(), precision=lax....]
    transpose x4 -> x0, local copies, waits for them, and re-layouts: 8.31 us -> none  [the longest x1 7.62 us: reduce_bias(): grad_sums.reshape(count, HEADS, zone, WIN_LON, zone, WIN_LON)]
    another operation x3 -> x0, local copies, waits for them, and re-layouts: 5.89 us -> none
    reshape x5 -> x0, local copies, waits for them, and re-layouts: 5.46 us -> none  [the longest x1 4.98 us: reduce_bias(): grad_sums.reshape(count, HEADS, zone, WIN_LON, zone, WIN_LON)]
  transfers between devices with their start and end apart: 6 -> 0, of which waited for: 2 -> 0; matrix products, arithmetic and copies ran while one was open for 44% -> 0% of each run, Pallas kernels for 0% -> 0%
where the time goes in v1:
time: 45.3 us; the launch traced here: 45.2 us
  Pallas kernels  42.6 us (94%)
  local copies, waits for them, and re-layouts  1.9 us (4%)
  between operations  0.64 us (1%)
    pallas_call x1, Pallas kernels, per_device(): pl.pallas_call(functools.partial(kernel, lat_size, lon_size, pairs_here),...  42.6 us
    unnamed x3, local copies, waits for them, and re-layouts  1.9 us

profile of v1, /device:TPU:6, one launch (start us, length us, event | category | flops | bytes accessed | tf_op | source)
XLA Modules:
  0.0 45.2 jit_solution(9752197082017944007)
XLA Ops:
  0.6 42.6 %shard_map.94 = (bf16[6,24,384]{2,1,0:T(8,128)(2,1)S(1)}, bf16[6,24,384]{2,1,0:T(8,128)(2,1)S(1)}, f32[6,9,1,23]{3,2,1,0:T(1,128)S(1)}) custom-call(bf16[6,24,384]{2,1,0:T(8,128)(2,1)} %fields_hbm.1, f32[1,192]{1,0:T(1,128)} %bitcast.5, bf16[192,576]{1,0:T(8,128)(2,1)} %win_hbm.1, bf16[192,192]{1,0:T(8,128)(2,1)} %wout_hbm.1, f32[6,9,1,23]{3,2,1,0:T(1,128)} %bitcast.4, ...), custom_call_target="tpu_custom_call" | custom-call | tf_op jit(solution)/shard_map/pallas_call | solution.py:492
  43.3 0.6 %copy.13 = bf16[6,24,384]{2,1,0:T(8,128)(2,1)} copy(bf16[6,24,384]{2,1,0:T(8,128)(2,1)S(1)} %get-tuple-element.12) | data formatting | bytes 221184
  43.9 0.6 %copy.14 = bf16[6,24,384]{2,1,0:T(8,128)(2,1)} copy(bf16[6,24,384]{2,1,0:T(8,128)(2,1)S(1)} %get-tuple-element.13) | data formatting | bytes 221184
  44.6 0.6 %copy.15 = f32[1,6,9,23]{3,0,2,1:T(1,128)} copy(f32[1,6,9,23]{3,0,2,1:T(1,128)S(1)} %bitcast.3) | data formatting | bytes 9936

commit v2 on v1

v2 whole, which is shorter than its diff:
```python
import functools

import jax
import jax.numpy as jnp
from jax import lax
from jax.experimental import pallas as pl
from jax.experimental.pallas import tpu as pltpu
from jax.sharding import PartitionSpec as P

WIDTH = 192
HEADS = 6
HEAD_DIM = 32
LEVELS = 2
WIN_LAT = 6
WIN_LON = 12
ZONE = LEVELS * WIN_LAT
CELLS = WIN_LAT * WIN_LON
TOKENS = LEVELS * CELLS
OFFSETS = 23
SLOT = 24
PAIRS = ZONE * ZONE
RIM_R = WIN_LAT // 2
RIM_C = WIN_LON // 2
WINDOWS = 2
COLS = WINDOWS * WIN_LON
FEATS = LEVELS * WIDTH
BAND = 384
BIG = 56
SMALL = 24
SCALE = HEAD_DIM**-0.5
EPS = 1e-05
MASKED = -1e30
MESH = pl.DeviceIdType.MESH
F32 = jnp.float32
BF16 = jnp.bfloat16


def dot_nn(a, b):
    return lax.dot_general(a, b, (((1,), (0,)), ((), ())), preferred_element_type=F32)


def dot_nt(a, b):
    return lax.dot_general(a, b, (((1,), (1,)), ((), ())), preferred_element_type=F32)


def dot_tn(a, b):
    return lax.dot_general(a, b, (((0,), (0,)), ((), ())), preferred_element_type=F32)


def kernel(
    lat_size,
    lon_size,
    pairs_here,
    fields_hbm,
    gain_hbm,
    win_hbm,
    wout_hbm,
    bias_hbm,
    pad_hbm,
    cot_hbm,
    out_ref,
    grads_ref,
    table_ref,
    f_in,
    c_in,
    w_in,
    wo_in,
    bias_in,
    gain_ref,
    pad_ref,
    raw,
    xw,
    tmp,
    send_big,
    send_small,
    in_big,
    in_small,
    res_big,
    res_small,
    back_big,
    back_small,
    bias_msg,
    bias_recv,
    spread,
    bias_flat,
    bias_full,
    w_t,
    xtok,
    ctok,
    xhat,
    spread_inv,
    proj_t,
    k_nat,
    v_nat,
    gmix_t,
    mixed_t,
    gproj_t,
    gflat,
    cells,
    table_msg,
    table_recv,
    selector,
    load_sem,
    halo_send,
    halo_recv,
    back_send,
    back_recv,
    bias_send,
    bias_rsem,
    table_send,
    table_rsem,
    ready_sem,
):
    lat = lax.axis_index("lat")
    lon = lax.axis_index("lon")
    up = lax.rem(lat + lat_size - 1, lat_size)
    dn = lax.rem(lat + 1, lat_size)
    lf = lax.rem(lon + lon_size - 1, lon_size)
    rt = lax.rem(lon + 1, lon_size)
    group = lat_size // 2
    place = lax.rem(lat, group)
    is_first = place == 0
    is_last = place == group - 1
    before_last = place == group - 2
    one_if_last = jnp.where(is_last, 1, 0)
    one_if_first = jnp.where(is_first, 1, 0)
    below = jnp.where(is_last, dn, lat)
    above = jnp.where(is_first, lat, up)

    barrier = pltpu.get_barrier_semaphore()

    def signal(dev):
        pl.semaphore_signal(barrier, inc=1, device_id=dev, device_id_type=MESH)

    def greet_seam(s, carry):
        signal((up, lax.rem(lon + s, lon_size)))
        return carry

    def greet(s, carry):
        signal((lat, lax.rem(lon + s, lon_size)))
        return carry

    @pl.when(is_first)
    def _():
        lax.fori_loop(0, lon_size, greet_seam, 0)

    @pl.when(jnp.logical_not(is_first))
    def _():
        signal((up, lon))
        signal((up, lf))

    @pl.when(jnp.logical_not(is_last))
    def _():
        signal((dn, lon))
        lax.fori_loop(1, lon_size, greet, 0)

    @pl.when(jnp.logical_not(is_last | before_last))
    def _():
        signal((dn, rt))

    loads = [
        pltpu.make_async_copy(src, dst, load_sem.at[n])
        for n, (src, dst) in enumerate(
            (
                (fields_hbm, f_in),
                (cot_hbm, c_in),
                (bias_hbm, bias_in),
                (win_hbm, w_in),
                (wout_hbm, wo_in),
                (gain_hbm, gain_ref),
                (pad_hbm, pad_ref),
            )
        )
    ]
    for load in loads:
        load.start()

    def remote(src, dst, send, recv, dev):
        return pltpu.make_async_remote_copy(
            src_ref=src,
            dst_ref=dst,
            send_sem=send,
            recv_sem=recv,
            device_id=dev,
            device_id_type=MESH,
        )

    def big_last(kind):
        return remote(
            send_big.at[kind, 0],
            in_big.at[kind, 1, 0],
            halo_send.at[kind, 0],
            halo_recv.at[kind, 1, 0],
            (dn, lon),
        )

    def big_up(kind):
        return remote(
            send_big.at[kind, 1],
            in_big.at[kind, 0, 1],
            halo_send.at[kind, 1],
            halo_recv.at[kind, 0, 0],
            (up, lon),
        )

    def small_low(kind):
        return remote(
            send_small.at[kind, 0],
            in_small.at[kind, one_if_last, 0],
            halo_send.at[kind, 2],
            halo_recv.at[kind, one_if_last, 1],
            (below, lf),
        )

    def small_top(kind):
        return remote(
            send_small.at[kind, 1],
            in_small.at[kind, one_if_first, 1],
            halo_send.at[kind, 3],
            halo_recv.at[kind, one_if_first, 2],
            (above, lf),
        )

    def wait_halo(kind, slot):
        remote(
            send_big.at[kind, 0],
            in_big.at[kind, slot, 1 - slot],
            halo_send.at[kind, 0],
            halo_recv.at[kind, slot, 0],
            (dn, lon),
        ).wait_recv()
        for half in range(2):
            remote(
                send_small.at[kind, half],
                in_small.at[kind, slot, half],
                halo_send.at[kind, 2],
                halo_recv.at[kind, slot, 1 + half],
                (dn, lon),
            ).wait_recv()

    def pack_in(src, kind):
        for r in range(WIN_LAT):
            raw[r * COLS : (r + 1) * COLS, :] = src[r].astype(F32)
        for half, first in ((0, RIM_R), (1, 0)):
            base, side = half * 88, 64 + half * 88
            for r in range(RIM_R):
                row = (first + r) * COLS
                tmp[base + r * 12 : base + r * 12 + 12, :] = raw[row + 6 : row + 18, :]
                tmp[base + 36 + r * 6 : base + 42 + r * 6, :] = raw[row + 18 : row + 24, :]
                tmp[side + r * 6 : side + 6 + r * 6, :] = raw[row : row + 6, :]
            piece = tmp[base : base + BIG, :].astype(BF16)
            send_big[kind, half] = piece
            in_big[kind, half, half] = piece
            send_small[kind, half] = tmp[side : side + SMALL, :].astype(BF16)

    def unpack_in(kind, slot):
        for half in range(2):
            base, side = half * 88, 64 + half * 88
            tmp[base : base + BIG, :] = in_big[kind, slot, half].astype(F32)
            tmp[side : side + SMALL, :] = in_small[kind, slot, half].astype(F32)
            xw[36 * half : 36 * half + 36, :] = tmp[base : base + 36, :]
            for r in range(RIM_R):
                row = CELLS + (RIM_R * half + r) * 12
                xw[row : row + 6, :] = tmp[base + 36 + r * 6 : base + 42 + r * 6, :]
                xw[row + 6 : row + 12, :] = tmp[side + r * 6 : side + 6 + r * 6, :]

    tmp[...] = jnp.zeros_like(tmp)
    loads[0].wait()
    pack_in(f_in, 0)
    loads[2].wait()
    bias_msg[...] = jnp.zeros_like(bias_msg)
    for r in range(pairs_here):
        for h in range(HEADS):
            bias_msg[h : h + 1, r * SLOT : r * SLOT + OFFSETS] = bias_in[h, r]
    bias_recv[0, lon] = bias_msg[...]
    loads[1].wait()
    pack_in(c_in, 1)

    pl.semaphore_wait(barrier, jnp.where(is_first | is_last, lon_size + 1, lon_size + 3))

    @pl.when(before_last)
    def _():
        pl.semaphore_signal(ready_sem, inc=1, device_id=(dn, rt), device_id_type=MESH)

    def bias_copy(s):
        return remote(
            bias_msg,
            bias_recv.at[one_if_last, lon],
            bias_send.at[s],
            bias_rsem.at[one_if_last, lon],
            (below, lax.rem(lon + s, lon_size)),
        )

    def bias_arrival(slot, s):
        source = lax.rem(lon + s, lon_size)
        return remote(
            bias_msg,
            bias_recv.at[slot, source],
            bias_send.at[s],
            bias_rsem.at[slot, source],
            (dn, lon),
        )

    def send_bias(s, carry):
        bias_copy(s).start()
        return carry

    for kind in range(2):

        @pl.when(is_last)
        def _():
            big_last(kind).start()

        small_low(kind).start()

        @pl.when(jnp.logical_not(is_first))
        def _():
            big_up(kind).start()

        @pl.when(jnp.logical_not(is_last))
        def _():
            small_top(kind).start()

        if kind == 0:
            lax.fori_loop(1 - one_if_last, lon_size, send_bias, 0)

    @pl.when(is_last)
    def _():
        pl.semaphore_wait(ready_sem, 1)
        for kind in range(2):
            small_top(kind).start()

    gflat[...] = jnp.zeros_like(gflat)
    table_msg[...] = jnp.zeros_like(table_msg)
    spread[...] = jnp.zeros_like(spread)
    lane = lax.broadcasted_iota(jnp.int32, (BAND, TOKENS), 0)
    query = lax.broadcasted_iota(jnp.int32, (BAND, TOKENS), 1)
    picked = (query // WIN_LON) * SLOT + query % WIN_LON + WIN_LON - 1
    selector[...] = (lane == picked).astype(F32).astype(BF16)
    loads[3].wait()
    loads[4].wait()
    loads[5].wait()
    loads[6].wait()
    w_t[...] = w_in[...].astype(F32).T.astype(BF16)
    total_rows = lat_size * WIN_LAT
    key_band = (lax.broadcasted_iota(jnp.int32, (TOKENS, TOKENS), 0) // WIN_LON) % WIN_LAT
    query_band = (lax.broadcasted_iota(jnp.int32, (TOKENS, TOKENS), 1) // WIN_LON) % WIN_LAT

    def back_copy_big(kind, slot):
        return remote(
            res_big.at[kind, slot, 1 - slot],
            back_big.at[kind, 1 - slot],
            back_send.at[kind, slot, 0],
            back_recv.at[kind, 1 - slot],
            (jnp.where(slot == 0, dn, up), lon),
        )

    def back_copy_small(kind, slot, half):
        owner = lax.rem(lat + half - slot + lat_size, lat_size)
        return remote(
            res_small.at[kind, slot, half],
            back_small.at[kind, half],
            back_send.at[kind, slot, 1 + half],
            back_recv.at[kind, 2 + half],
            (owner, rt),
        )

    def give_back(kind, slot, tokens):
        for w in range(WINDOWS):
            cells[w * CELLS : (w + 1) * CELLS, 0:WIDTH] = tokens[w][0:CELLS]
            cells[w * CELLS : (w + 1) * CELLS, WIDTH:] = tokens[w][CELLS:]
        for half in range(2):
            base, side = half * 88, 64 + half * 88
            tmp[base : base + 36, :] = cells[36 * half : 36 * half + 36, :]
            for r in range(RIM_R):
                row = CELLS + (RIM_R * half + r) * 12
                tmp[base + 36 + r * 6 : base + 42 + r * 6, :] = cells[row : row + 6, :]
                tmp[side + r * 6 : side + 6 + r * 6, :] = cells[row + 6 : row + 12, :]
            res_big[kind, slot, half] = tmp[base : base + BIG, :].astype(BF16)
            res_small[kind, slot, half] = tmp[side : side + SMALL, :].astype(BF16)
        for half in range(2):
            back_copy_small(kind, slot, half).start()
        back_copy_big(kind, slot).start()
        back_big[kind, slot] = res_big[kind, slot, slot]

    def table_copy(slot, s):
        peer = lax.rem(lon + s, lon_size)
        return remote(
            table_msg.at[slot, peer],
            table_recv.at[lon],
            table_send.at[slot, s],
            table_rsem.at[lon],
            (jnp.where(slot == 0, lat, up), peer),
        )

    def table_arrival(s):
        source = lax.rem(lon + s, lon_size)
        return remote(
            table_msg.at[0, source],
            table_recv.at[source],
            table_send.at[0, s],
            table_rsem.at[source],
            (lat, source),
        )

    def window_row(slot, carry):
        gain = gain_ref[...]
        wait_halo(0, slot)
        unpack_in(0, slot)
        for w in range(WINDOWS):
            block = xw[w * CELLS : (w + 1) * CELLS, :]
            x = jnp.concatenate([block[:, :WIDTH], block[:, WIDTH:]], axis=0)
            xtok[w] = x
            center = x - jnp.mean(x, axis=1, keepdims=True)
            inverse = lax.rsqrt(jnp.mean(center * center, axis=1, keepdims=True) + EPS)
            normed = center * inverse
            xhat[w] = normed
            spread_inv[w] = inverse
            x_n = (normed * gain).astype(BF16)
            proj_t[w] = dot_nt(w_t[...], x_n).astype(BF16)
            kv = dot_nn(x_n, w_in[:, WIDTH:]).astype(BF16)
            for h in range(HEADS):
                k_nat[w, h] = kv[:, h * HEAD_DIM : (h + 1) * HEAD_DIM]
                v_nat[w, h] = kv[:, WIDTH + h * HEAD_DIM : WIDTH + (h + 1) * HEAD_DIM]
        wait_halo(1, slot)
        unpack_in(1, slot)
        for w in range(WINDOWS):
            block = xw[w * CELLS : (w + 1) * CELLS, :]
            c = jnp.concatenate([block[:, :WIDTH], block[:, WIDTH:]], axis=0)
            ctok[w] = c
            gmix_t[w] = dot_nt(wo_in[...], c.astype(BF16)).astype(BF16)

        first_row = jnp.where(slot == 0, lat, up) * WIN_LAT + RIM_R
        key_row = lax.rem(first_row + key_band, total_rows)
        query_row = lax.rem(first_row + query_band, total_rows)
        real = jnp.zeros((TOKENS, TOKENS), jnp.int32)
        for a in range(WIN_LAT):
            real = jnp.where(key_band == a, pad_ref[lax.rem(first_row + a, total_rows)], real)
        allowed = (jnp.abs(query_row - key_row) < WIN_LAT) & (real == 1)

        def wait_bias(s, inner):
            bias_arrival(slot, s).wait_recv()
            return inner

        lax.fori_loop(1 - slot, lon_size, wait_bias, 0)
        for p in range(PAIRS):
            owner, r = p // pairs_here, p % pairs_here
            zq, zt = p // ZONE, p % ZONE
            spread[zt * 8 : zt * 8 + 8, zq * SLOT : (zq + 1) * SLOT] = bias_recv[
                slot, owner, :, r * SLOT : (r + 1) * SLOT
            ]
        for b in range(WIN_LON):
            table = spread[...]
            if b:
                table = pltpu.roll(table, b, 1)
            high = table.astype(BF16)
            rest = table - high.astype(F32)
            middle = rest.astype(BF16)
            low = (rest - middle.astype(F32)).astype(BF16)
            pick = selector[...]
            wide = dot_nn(high, pick) + (dot_nn(middle, pick) + dot_nn(low, pick))
            for zt in range(ZONE):
                row = (zt * WIN_LON + b) * 8
                bias_flat[0, row : row + 8, :] = wide[zt * 8 : zt * 8 + 8, 0:128]
                bias_flat[1, row : row + 8, 0 : TOKENS - 128] = wide[
                    zt * 8 : zt * 8 + 8, 128:TOKENS
                ]
        for h in range(HEADS):
            left = bias_flat[0, pl.ds(h, TOKENS, stride=8), :]
            right = bias_flat[1, pl.ds(h, TOKENS, stride=8), :]
            whole = jnp.concatenate([left, right[:, 0 : TOKENS - 128]], axis=1)
            bias_full[h] = jnp.where(allowed, whole, MASKED)

        for h in range(HEADS):
            at_q = pl.ds(h * HEAD_DIM, HEAD_DIM)
            at_k = pl.ds(WIDTH + h * HEAD_DIM, HEAD_DIM)
            at_v = pl.ds(2 * WIDTH + h * HEAD_DIM, HEAD_DIM)
            bias = bias_full[h]
            summed = None
            for w in range(WINDOWS):
                q_t = proj_t[w, at_q, :]
                g_t = gmix_t[w, at_q, :]
                scores = dot_nn(k_nat[w, h], q_t) * SCALE + bias
                raised = jnp.exp(scores - jnp.max(scores, axis=0, keepdims=True))
                weights = raised * (1.0 / jnp.sum(raised, axis=0, keepdims=True))
                weights_low = weights.astype(BF16)
                mixed_t[w, at_q, :] = dot_nn(proj_t[w, at_v, :], weights_low).astype(BF16)
                grad_w = dot_nn(v_nat[w, h], g_t)
                grad_s = weights * (grad_w - jnp.sum(weights * grad_w, axis=0, keepdims=True))
                grad_low = grad_s.astype(BF16)
                gproj_t[w, at_q, :] = (dot_nn(proj_t[w, at_k, :], grad_low) * SCALE).astype(BF16)
                gproj_t[w, at_k, :] = (dot_nt(q_t, grad_low) * SCALE).astype(BF16)
                gproj_t[w, at_v, :] = dot_nt(g_t, weights_low).astype(BF16)
                summed = grad_s if summed is None else summed + grad_s
            gflat[0, pl.ds(h, TOKENS, stride=8), :] = summed[:, 0:128]
            gflat[1, pl.ds(h, TOKENS, stride=8), 0 : TOKENS - 128] = summed[:, 128:TOKENS]

        give_back(
            0, slot, [xtok[w] + dot_tn(mixed_t[w], wo_in[...]) for w in range(WINDOWS)]
        )
        grads = []
        for w in range(WINDOWS):
            scaled = dot_tn(gproj_t[w], w_t[...]) * gain
            normed = xhat[w]
            centered = (
                scaled
                - jnp.mean(scaled, axis=1, keepdims=True)
                - normed * jnp.mean(scaled * normed, axis=1, keepdims=True)
            )
            grads.append(ctok[w] + spread_inv[w] * centered)
        give_back(1, slot, grads)

        total = jnp.zeros((ZONE * 8, BAND), F32)
        for b in range(WIN_LON):
            picked_rows = []
            for zt in range(ZONE):
                row = (zt * WIN_LON + b) * 8
                picked_rows.append(
                    jnp.concatenate(
                        [
                            gflat[0, row : row + 8, :],
                            gflat[1, row : row + 8, 0 : TOKENS - 128],
                        ],
                        axis=1,
                    )
                )
            part = jnp.concatenate(picked_rows, axis=0)
            high = part.astype(BF16)
            low = (part - high.astype(F32)).astype(BF16)
            placed = dot_nt(high, selector[...]) + dot_nt(low, selector[...])
            if b:
                placed = pltpu.roll(placed, BAND - b, 1)
            total = total + placed
        spread[...] = total
        for p in range(PAIRS):
            owner, r = p // pairs_here, p % pairs_here
            zq, zt = p // ZONE, p % ZONE
            table_msg[slot, owner, :, r * SLOT : (r + 1) * SLOT] = spread[
                zt * 8 : zt * 8 + 8, zq * SLOT : (zq + 1) * SLOT
            ]

        def send_table(s, inner):
            table_copy(slot, s).start()
            return inner

        lax.fori_loop(1 - slot, lon_size, send_table, 0)

        @pl.when(slot == 0)
        def _():
            table_recv[lon] = table_msg[0, lon]

        return carry

    rows_here = 1 + one_if_first - one_if_last
    lax.fori_loop(0, rows_here, window_row, 0)

    def take_back(kind, dst):
        def arrived_big(half):
            remote(
                res_big.at[kind, 0, half],
                back_big.at[kind, half],
                back_send.at[kind, 0, 0],
                back_recv.at[kind, half],
                (dn, lon),
            ).wait_recv()

        @pl.when(is_last)
        def _():
            arrived_big(0)

        @pl.when(jnp.logical_not(is_first))
        def _():
            arrived_big(1)

        for half in range(2):
            remote(
                res_small.at[kind, 0, half],
                back_small.at[kind, half],
                back_send.at[kind, 0, 1],
                back_recv.at[kind, 2 + half],
                (dn, rt),
            ).wait_recv()
        for half, first in ((0, RIM_R), (1, 0)):
            base, side = half * 88, 64 + half * 88
            tmp[base : base + BIG, :] = back_big[kind, half].astype(F32)
            tmp[side : side + SMALL, :] = back_small[kind, half].astype(F32)
            for r in range(RIM_R):
                row = (first + r) * COLS
                raw[row + 6 : row + 18, :] = tmp[base + r * 12 : base + r * 12 + 12, :]
                raw[row + 18 : row + 24, :] = tmp[base + 36 + r * 6 : base + 42 + r * 6, :]
                raw[row : row + 6, :] = tmp[side + r * 6 : side + 6 + r * 6, :]
        for r in range(WIN_LAT):
            dst[r] = raw[r * COLS : (r + 1) * COLS, :].astype(BF16)

    take_back(0, out_ref)
    take_back(1, grads_ref)

    def wait_table(s, carry):
        table_arrival(s).wait_recv()
        return carry

    lax.fori_loop(1 - one_if_last, lon_size, wait_table, 0)
    added = table_recv[0]
    for j in range(1, lon_size):
        added = added + table_recv[j]
    for r in range(pairs_here):
        piece = added[:, r * SLOT : r * SLOT + OFFSETS]
        for h in range(HEADS):
            table_ref[h, r] = piece[h : h + 1, :]

    for kind in range(2):

        @pl.when(is_last)
        def _():
            big_last(kind).wait_send()

        @pl.when(jnp.logical_not(is_first))
        def _():
            big_up(kind).wait_send()

        small_low(kind).wait_send()
        small_top(kind).wait_send()

    def drain_bias(s, carry):
        bias_copy(s).wait_send()
        return carry

    lax.fori_loop(1 - one_if_last, lon_size, drain_bias, 0)

    def drain_row(slot, carry):
        for kind in range(2):
            back_copy_big(kind, slot).wait_send()
            for half in range(2):
                back_copy_small(kind, slot, half).wait_send()

        def drain_table(s, inner):
            table_copy(slot, s).wait_send()
            return inner

        lax.fori_loop(1 - slot, lon_size, drain_table, 0)
        return carry

    lax.fori_loop(0, rows_here, drain_row, 0)


def place_out(*refs):
    sources, targets, sem = refs[:3], refs[3:6], refs[6]
    copies = [
        pltpu.make_async_copy(src, dst, sem.at[n])
        for n, (src, dst) in enumerate(zip(sources, targets))
    ]
    for copy in copies:
        copy.start()
    for copy in copies:
        copy.wait()


def solution(mesh):
    lat_size, lon_size = mesh.shape["lat"], mesh.shape["lon"]
    pairs_here = PAIRS // lon_size
    lanes = -(-pairs_here * SLOT // 128) * 128

    def per_device(fields, norm_gain, project_in, project_out, bias_table, pad_rows, cotangent):
        hbm_spec = pl.BlockSpec(memory_space=pltpu.HBM)
        vmem_spec = pl.BlockSpec(memory_space=pltpu.VMEM)
        out_fields, field_grads, table_grads = pl.pallas_call(
            functools.partial(kernel, lat_size, lon_size, pairs_here),
            out_shape=(
                jax.ShapeDtypeStruct(fields.shape, BF16),
                jax.ShapeDtypeStruct(fields.shape, BF16),
                jax.ShapeDtypeStruct((HEADS, pairs_here, 1, OFFSETS), F32),
            ),
            in_specs=[hbm_spec] * 7,
            out_specs=(vmem_spec, vmem_spec, vmem_spec),
            scratch_shapes=[
                pltpu.VMEM(fields.shape, BF16),
                pltpu.VMEM(fields.shape, BF16),
                pltpu.VMEM(project_in.shape, BF16),
                pltpu.VMEM(project_out.shape, BF16),
                pltpu.VMEM((HEADS, pairs_here, 1, OFFSETS), F32),
                pltpu.VMEM((1, WIDTH), F32),
                pltpu.SMEM(pad_rows.shape, jnp.int32),
                pltpu.VMEM((WIN_LAT * COLS, FEATS), F32),
                pltpu.VMEM((WINDOWS * CELLS, FEATS), F32),
                pltpu.VMEM((176, FEATS), F32),
                pltpu.VMEM((2, 2, BIG, FEATS), BF16),
                pltpu.VMEM((2, 2, SMALL, FEATS), BF16),
                pltpu.VMEM((2, 2, 2, BIG, FEATS), BF16),
                pltpu.VMEM((2, 2, 2, SMALL, FEATS), BF16),
                pltpu.VMEM((2, 2, 2, BIG, FEATS), BF16),
                pltpu.VMEM((2, 2, 2, SMALL, FEATS), BF16),
                pltpu.VMEM((2, 2, BIG, FEATS), BF16),
                pltpu.VMEM((2, 2, SMALL, FEATS), BF16),
                pltpu.VMEM((8, lanes), F32),
                pltpu.VMEM((2, lon_size, 8, lanes), F32),
                pltpu.VMEM((ZONE * 8, BAND), F32),
                pltpu.VMEM((2, TOKENS * 8, 128), F32),
                pltpu.VMEM((HEADS, TOKENS, TOKENS), F32),
                pltpu.VMEM((3 * WIDTH, WIDTH), BF16),
                pltpu.VMEM((WINDOWS, TOKENS, WIDTH), F32),
                pltpu.VMEM((WINDOWS, TOKENS, WIDTH), F32),
                pltpu.VMEM((WINDOWS, TOKENS, WIDTH), F32),
                pltpu.VMEM((WINDOWS, TOKENS, 1), F32),
                pltpu.VMEM((WINDOWS, 3 * WIDTH, TOKENS), BF16),
                pltpu.VMEM((WINDOWS, HEADS, TOKENS, HEAD_DIM), BF16),
                pltpu.VMEM((WINDOWS, HEADS, TOKENS, HEAD_DIM), BF16),
                pltpu.VMEM((WINDOWS, WIDTH, TOKENS), BF16),
                pltpu.VMEM((WINDOWS, WIDTH, TOKENS), BF16),
                pltpu.VMEM((WINDOWS, 3 * WIDTH, TOKENS), BF16),
                pltpu.VMEM((2, TOKENS * 8, 128), F32),
                pltpu.VMEM((WINDOWS * CELLS, FEATS), F32),
                pltpu.VMEM((2, lon_size, 8, lanes), F32),
                pltpu.VMEM((lon_size, 8, lanes), F32),
                pltpu.VMEM((BAND, TOKENS), BF16),
                pltpu.SemaphoreType.DMA((7,)),
                pltpu.SemaphoreType.DMA((2, 4)),
                pltpu.SemaphoreType.DMA((2, 2, 3)),
                pltpu.SemaphoreType.DMA((2, 2, 3)),
                pltpu.SemaphoreType.DMA((2, 4)),
                pltpu.SemaphoreType.DMA((lon_size,)),
                pltpu.SemaphoreType.DMA((2, lon_size)),
                pltpu.SemaphoreType.DMA((2, lon_size)),
                pltpu.SemaphoreType.DMA((lon_size,)),
                pltpu.SemaphoreType.REGULAR,
            ],
            compiler_params=pltpu.CompilerParams(
                collective_id=0, has_side_effects=True, vmem_limit_bytes=48 << 20
            ),
        )(
            *(
                pltpu.with_memory_space_constraint(x, pltpu.HBM)
                for x in (
                    fields,
                    norm_gain.reshape(1, WIDTH),
                    project_in,
                    project_out,
                    bias_table.reshape(HEADS, pairs_here, 1, OFFSETS),
                    pad_rows,
                    cotangent,
                )
            )
        )
        parts = (out_fields, field_grads, table_grads)
        any_spec = pl.BlockSpec(memory_space=pl.ANY)
        out_fields, field_grads, table_grads = pl.pallas_call(
            place_out,
            out_shape=tuple(jax.ShapeDtypeStruct(x.shape, x.dtype) for x in parts),
            in_specs=[any_spec] * 3,
            out_specs=(hbm_spec,) * 3,
            scratch_shapes=[pltpu.SemaphoreType.DMA((3,))],
            compiler_params=pltpu.CompilerParams(vmem_limit_bytes=1 << 20),
        )(*parts)
        return out_fields, field_grads, table_grads.reshape(bias_table.shape)

    in_specs = (
        P("lat", "lon", None),
        P(),
        P(),
        P(),
        P("lat", None, "lon", None),
        P(),
        P("lat", "lon", None),
    )
    out_specs = (P("lat", "lon", None), P("lat", "lon", None), P("lat", None, "lon", None))
    return jax.shard_map(
        per_device, mesh=mesh, in_specs=in_specs, out_specs=out_specs, check_vma=False
    )
```

time: 45.3 us -> 49.4 us (1.091)
  Pallas kernels: 42.6 us -> 48.6 us
  local copies, waits for them, and re-layouts: 1.9 us -> 0 us
    pallas_call x1, Pallas kernels: 42.6 us -> 47.9 us  [per_device(): pl.pallas_call(functools.partial(kernel, lat_size, lon_size, pairs_here),...]
    unnamed x3 -> x0, local copies, waits for them, and re-layouts: 1.9 us -> none
    pallas_call x0 -> x1, Pallas kernels: none -> 0.71 us  [per_device(): pl.pallas_call(place_out, out_shape=tuple((jax.ShapeDtypeStruct(x.shape,...]
where the time goes in v2:
time: 49.4 us; the launch traced here: 49.3 us
  Pallas kernels  48.6 us (98%)
  between operations  0.64 us (1%)
    pallas_call x1, Pallas kernels, per_device(): pl.pallas_call(functools.partial(kernel, lat_size, lon_size, pairs_here),...  47.9 us

profile of v2, /device:TPU:6, one launch (start us, length us, event | category | flops | bytes accessed | tf_op | source)
XLA Modules:
  0.0 49.3 jit_solution(18369941982100348955)
XLA Ops:
  0.6 47.9 %shard_map.94 = (bf16[6,24,384]{2,1,0:T(8,128)(2,1)S(1)}, bf16[6,24,384]{2,1,0:T(8,128)(2,1)S(1)}, f32[6,9,1,23]{3,2,1,0:T(1,128)S(1)}) custom-call(bf16[6,24,384]{2,1,0:T(8,128)(2,1)} %fields_hbm.1, f32[1,192]{1,0:T(1,128)} %bitcast.4, bf16[192,576]{1,0:T(8,128)(2,1)} %win_hbm.1, bf16[192,192]{1,0:T(8,128)(2,1)} %wout_hbm.1, f32[6,9,1,23]{3,2,1,0:T(1,128)} %bitcast.3, ...), custom_call_target="tpu_custom_call" | custom-call | tf_op jit(solution)/shard_map/pallas_call | solution.py:666
  48.6 0.7 %shard_map.95 = (bf16[6,24,384]{2,1,0:T(8,128)(2,1)}, bf16[6,24,384]{2,1,0:T(8,128)(2,1)}, f32[6,9,1,23]{3,2,1,0:T(1,128)}) custom-call(bf16[6,24,384]{2,1,0:T(8,128)(2,1)S(1)} %get-tuple-element.9.refs_0_, bf16[6,24,384]{2,1,0:T(8,128)(2,1)S(1)} %get-tuple-element.10.refs_1_, f32[6,9,1,23]{3,2,1,0:T(1,128)S(1)} %get-tuple-element.11.refs_2_), custom_call_target="tpu_custom_call" | custom-call | tf_op jit(solution)/shard_map/pallas_call | solution.py:745

commit v3 on v2

--- a/solution.py
+++ b/solution.py
@@ -99,7 +99,12 @@
     cells,
     table_msg,
     table_recv,
-    selector,
+    spreader,
+    gatherer,
+    score_buf,
+    gw_buf,
+    p_low,
+    d_low,
     load_sem,
     halo_send,
     halo_recv,
@@ -162,9 +167,9 @@
         pltpu.make_async_copy(src, dst, load_sem.at[n])
         for n, (src, dst) in enumerate(
             (
+                (bias_hbm, bias_in),
                 (fields_hbm, f_in),
                 (cot_hbm, c_in),
-                (bias_hbm, bias_in),
                 (win_hbm, w_in),
                 (wout_hbm, wo_in),
                 (gain_hbm, gain_ref),
@@ -265,16 +270,14 @@
                 xw[row + 6 : row + 12, :] = tmp[side + r * 6 : side + 6 + r * 6, :]
 
     tmp[...] = jnp.zeros_like(tmp)
+    bias_msg[...] = jnp.zeros_like(bias_msg)
     loads[0].wait()
-    pack_in(f_in, 0)
-    loads[2].wait()
-    bias_msg[...] = jnp.zeros_like(bias_msg)
     for r in range(pairs_here):
         for h in range(HEADS):
             bias_msg[h : h + 1, r * SLOT : r * SLOT + OFFSETS] = bias_in[h, r]
     bias_recv[0, lon] = bias_msg[...]
     loads[1].wait()
-    pack_in(c_in, 1)
+    pack_in(f_in, 0)
 
     pl.semaphore_wait(barrier, jnp.where(is_first | is_last, lon_size + 1, lon_size + 3))
 
@@ -305,8 +308,7 @@
         bias_copy(s).start()
         return carry
 
-    for kind in range(2):
-
+    def send_halo(kind):
         @pl.when(is_last)
         def _():
             big_last(kind).start()
@@ -321,8 +323,11 @@
         def _():
             small_top(kind).start()
 
-        if kind == 0:
-            lax.fori_loop(1 - one_if_last, lon_size, send_bias, 0)
+    lax.fori_loop(1 - one_if_last, lon_size, send_bias, 0)
+    send_halo(0)
+    loads[2].wait()
+    pack_in(c_in, 1)
+    send_halo(1)
 
     @pl.when(is_last)
     def _():
@@ -333,10 +338,19 @@
     gflat[...] = jnp.zeros_like(gflat)
     table_msg[...] = jnp.zeros_like(table_msg)
     spread[...] = jnp.zeros_like(spread)
-    lane = lax.broadcasted_iota(jnp.int32, (BAND, TOKENS), 0)
-    query = lax.broadcasted_iota(jnp.int32, (BAND, TOKENS), 1)
-    picked = (query // WIN_LON) * SLOT + query % WIN_LON + WIN_LON - 1
-    selector[...] = (lane == picked).astype(F32).astype(BF16)
+
+    def make_selectors(b, carry):
+        lane = lax.broadcasted_iota(jnp.int32, (BAND, TOKENS), 0)
+        query = lax.broadcasted_iota(jnp.int32, (BAND, TOKENS), 1)
+        picked = (query // WIN_LON) * SLOT + query % WIN_LON + WIN_LON - 1 - b
+        spreader[b] = (lane == picked).astype(F32).astype(BF16)
+        lane = lax.broadcasted_iota(jnp.int32, (TOKENS, BAND), 1)
+        query = lax.broadcasted_iota(jnp.int32, (TOKENS, BAND), 0)
+        picked = (query // WIN_LON) * SLOT + query % WIN_LON + WIN_LON - 1 - b
+        gatherer[b] = (lane == picked).astype(F32).astype(BF16)
+        return carry
+
+    lax.fori_loop(0, WIN_LON, make_selectors, 0)
     loads[3].wait()
     loads[4].wait()
     loads[5].wait()
@@ -449,16 +463,16 @@
             spread[zt * 8 : zt * 8 + 8, zq * SLOT : (zq + 1) * SLOT] = bias_recv[
                 slot, owner, :, r * SLOT : (r + 1) * SLOT
             ]
+        table = spread[...]
+        high = table.astype(BF16)
+        rest = table - high.astype(F32)
+        middle = rest.astype(BF16)
+        low = (rest - middle.astype(F32)).astype(BF16)
+        rows = ZONE * 8
+        stacked = jnp.concatenate([high, middle, low], axis=0)
         for b in range(WIN_LON):
-            table = spread[...]
-            if b:
-                table = pltpu.roll(table, b, 1)
-            high = table.astype(BF16)
-            rest = table - high.astype(F32)
-            middle = rest.astype(BF16)
-            low = (rest - middle.astype(F32)).astype(BF16)
-            pick = selector[...]
-            wide = dot_nn(high, pick) + (dot_nn(middle, pick) + dot_nn(low, pick))
+            three = dot_nn(stacked, spreader[b])
+            wide = three[0:rows] + (three[rows : 2 * rows] + three[2 * rows :])
             for zt in range(ZONE):
                 row = (zt * WIN_LON + b) * 8
                 bias_flat[0, row : row + 8, :] = wide[zt * 8 : zt * 8 + 8, 0:128]
@@ -471,29 +485,42 @@
             whole = jnp.concatenate([left, right[:, 0 : TOKENS - 128]], axis=1)
             bias_full[h] = jnp.where(allowed, whole, MASKED)
 
+        def rows_of(part, h):
+            return pl.ds(part * WIDTH + h * HEAD_DIM, HEAD_DIM)
+
         for h in range(HEADS):
-            at_q = pl.ds(h * HEAD_DIM, HEAD_DIM)
-            at_k = pl.ds(WIDTH + h * HEAD_DIM, HEAD_DIM)
-            at_v = pl.ds(2 * WIDTH + h * HEAD_DIM, HEAD_DIM)
-            bias = bias_full[h]
+            for w in range(WINDOWS):
+                score_buf[w, h] = (
+                    dot_nn(k_nat[w, h], proj_t[w, rows_of(0, h), :]) * SCALE + bias_full[h]
+                )
+                gw_buf[w, h] = dot_nn(v_nat[w, h], gmix_t[w, rows_of(0, h), :])
+        for h in range(HEADS):
             summed = None
             for w in range(WINDOWS):
-                q_t = proj_t[w, at_q, :]
-                g_t = gmix_t[w, at_q, :]
-                scores = dot_nn(k_nat[w, h], q_t) * SCALE + bias
+                scores = score_buf[w, h]
                 raised = jnp.exp(scores - jnp.max(scores, axis=0, keepdims=True))
                 weights = raised * (1.0 / jnp.sum(raised, axis=0, keepdims=True))
-                weights_low = weights.astype(BF16)
-                mixed_t[w, at_q, :] = dot_nn(proj_t[w, at_v, :], weights_low).astype(BF16)
-                grad_w = dot_nn(v_nat[w, h], g_t)
+                p_low[w, h] = weights.astype(BF16)
+                grad_w = gw_buf[w, h]
                 grad_s = weights * (grad_w - jnp.sum(weights * grad_w, axis=0, keepdims=True))
-                grad_low = grad_s.astype(BF16)
-                gproj_t[w, at_q, :] = (dot_nn(proj_t[w, at_k, :], grad_low) * SCALE).astype(BF16)
-                gproj_t[w, at_k, :] = (dot_nt(q_t, grad_low) * SCALE).astype(BF16)
-                gproj_t[w, at_v, :] = dot_nt(g_t, weights_low).astype(BF16)
+                d_low[w, h] = grad_s.astype(BF16)
                 summed = grad_s if summed is None else summed + grad_s
             gflat[0, pl.ds(h, TOKENS, stride=8), :] = summed[:, 0:128]
             gflat[1, pl.ds(h, TOKENS, stride=8), 0 : TOKENS - 128] = summed[:, 128:TOKENS]
+        for h in range(HEADS):
+            for w in range(WINDOWS):
+                q_t = proj_t[w, rows_of(0, h), :]
+                g_t = gmix_t[w, rows_of(0, h), :]
+                weights_low = p_low[w, h]
+                grad_low = d_low[w, h]
+                mixed_t[w, rows_of(0, h), :] = dot_nn(
+                    proj_t[w, rows_of(2, h), :], weights_low
+                ).astype(BF16)
+                gproj_t[w, rows_of(0, h), :] = (
+                    dot_nn(proj_t[w, rows_of(1, h), :], grad_low) * SCALE
+                ).astype(BF16)
+                gproj_t[w, rows_of(1, h), :] = (dot_nt(q_t, grad_low) * SCALE).astype(BF16)
+                gproj_t[w, rows_of(2, h), :] = dot_nt(g_t, weights_low).astype(BF16)
 
         give_back(
             0, slot, [xtok[w] + dot_tn(mixed_t[w], wo_in[...]) for w in range(WINDOWS)]
@@ -524,13 +551,8 @@
                         axis=1,
                     )
                 )
-            part = jnp.concatenate(picked_rows, axis=0)
-            high = part.astype(BF16)
-            low = (part - high.astype(F32)).astype(BF16)
-            placed = dot_nt(high, selector[...]) + dot_nt(low, selector[...])
-            if b:
-                placed = pltpu.roll(placed, BAND - b, 1)
-            total = total + placed
+            part = jnp.concatenate(picked_rows, axis=0).astype(BF16)
+            total = total + dot_nn(part, gatherer[b])
         spread[...] = total
         for p in range(PAIRS):
             owner, r = p // pairs_here, p % pairs_here
@@ -711,7 +733,12 @@
                 pltpu.VMEM((WINDOWS * CELLS, FEATS), F32),
                 pltpu.VMEM((2, lon_size, 8, lanes), F32),
                 pltpu.VMEM((lon_size, 8, lanes), F32),
-                pltpu.VMEM((BAND, TOKENS), BF16),
+                pltpu.VMEM((WIN_LON, BAND, TOKENS), BF16),
+                pltpu.VMEM((WIN_LON, TOKENS, BAND), BF16),
+                pltpu.VMEM((WINDOWS, HEADS, TOKENS, TOKENS), F32),
+                pltpu.VMEM((WINDOWS, HEADS, TOKENS, TOKENS), F32),
+                pltpu.VMEM((WINDOWS, HEADS, TOKENS, TOKENS), BF16),
+                pltpu.VMEM((WINDOWS, HEADS, TOKENS, TOKENS), BF16),
                 pltpu.SemaphoreType.DMA((7,)),
                 pltpu.SemaphoreType.DMA((2, 4)),
                 pltpu.SemaphoreType.DMA((2, 2, 3)),

time: 49.4 us -> 41.4 us (0.84)
  Pallas kernels: 48.6 us -> 40.6 us
    pallas_call x1, Pallas kernels: 47.9 us -> 39.9 us  [per_device(): pl.pallas_call(functools.partial(kernel, lat_size, lon_size, pairs_here),...]
where the time goes in v3:
time: 41.4 us; the launch traced here: 41.2 us
  Pallas kernels  40.6 us (98%)
  between operations  0.64 us (2%)
    pallas_call x1, Pallas kernels, per_device(): pl.pallas_call(functools.partial(kernel, lat_size, lon_size, pairs_here),...  39.9 us

profile of v3, /device:TPU:6, one launch (start us, length us, event | category | flops | bytes accessed | tf_op | source)
XLA Modules:
  0.0 41.2 jit_solution(9643687504129942047)
XLA Ops:
  0.6 39.9 %shard_map.94 = (bf16[6,24,384]{2,1,0:T(8,128)(2,1)S(1)}, bf16[6,24,384]{2,1,0:T(8,128)(2,1)S(1)}, f32[6,9,1,23]{3,2,1,0:T(1,128)S(1)}) custom-call(bf16[6,24,384]{2,1,0:T(8,128)(2,1)} %fields_hbm.1, f32[1,192]{1,0:T(1,128)} %bitcast.4, bf16[192,576]{1,0:T(8,128)(2,1)} %win_hbm.1, bf16[192,192]{1,0:T(8,128)(2,1)} %wout_hbm.1, f32[6,9,1,23]{3,2,1,0:T(1,128)} %bitcast.3, ...), custom_call_target="tpu_custom_call" | custom-call | tf_op jit(solution)/shard_map/pallas_call | solution.py:688
  40.5 0.7 %shard_map.95 = (bf16[6,24,384]{2,1,0:T(8,128)(2,1)}, bf16[6,24,384]{2,1,0:T(8,128)(2,1)}, f32[6,9,1,23]{3,2,1,0:T(1,128)}) custom-call(bf16[6,24,384]{2,1,0:T(8,128)(2,1)S(1)} %get-tuple-element.9.refs_0_, bf16[6,24,384]{2,1,0:T(8,128)(2,1)S(1)} %get-tuple-element.10.refs_1_, f32[6,9,1,23]{3,2,1,0:T(1,128)S(1)} %get-tuple-element.11.refs_2_), custom_call_target="tpu_custom_call" | custom-call | tf_op jit(solution)/shard_map/pallas_call | solution.py:772

commit v4 on v3

--- a/solution.py
+++ b/solution.py
@@ -27,6 +27,7 @@
 BAND = 384
 BIG = 56
 SMALL = 24
+RUN = 4
 SCALE = HEAD_DIM**-0.5
 EPS = 1e-05
 MASKED = -1e30
@@ -98,6 +99,8 @@
     gflat,
     cells,
     table_msg,
+    table_mid,
+    table_out,
     table_recv,
     spreader,
     gatherer,
@@ -112,6 +115,10 @@
     back_recv,
     bias_send,
     bias_rsem,
+    pass_send,
+    pass_recv,
+    table_xsend,
+    table_xrecv,
     table_send,
     table_rsem,
     ready_sem,
@@ -129,6 +136,11 @@
     before_last = place == group - 2
     one_if_last = jnp.where(is_last, 1, 0)
     one_if_first = jnp.where(is_first, 1, 0)
+    steps = lon_size // RUN
+    column = lon // RUN
+    inside = lax.rem(lon, RUN)
+    at_start = inside == 0
+    at_end = inside == RUN - 1
     below = jnp.where(is_last, dn, lat)
     above = jnp.where(is_first, lat, up)
 
@@ -141,9 +153,11 @@
         signal((up, lax.rem(lon + s, lon_size)))
         return carry
 
-    def greet(s, carry):
-        signal((lat, lax.rem(lon + s, lon_size)))
-        return carry
+    def run_peer(s):
+        return column * RUN + lax.rem(inside + s, RUN)
+
+    def column_peer(s):
+        return lax.rem(column + s, steps)
 
     @pl.when(is_first)
     def _():
@@ -157,7 +171,18 @@
     @pl.when(jnp.logical_not(is_last))
     def _():
         signal((dn, lon))
-        lax.fori_loop(1, lon_size, greet, 0)
+        for s in range(1, RUN):
+            signal((lat, run_peer(s)))
+        for s in range(1, steps):
+            signal((lat, column_peer(s) * RUN + inside))
+
+    @pl.when(jnp.logical_not(is_last) & at_start)
+    def _():
+        signal((lat, lf))
+
+    @pl.when(jnp.logical_not(is_last) & at_end)
+    def _():
+        signal((lat, rt))
 
     @pl.when(jnp.logical_not(is_last | before_last))
     def _():
@@ -279,7 +304,9 @@
     loads[1].wait()
     pack_in(f_in, 0)
 
-    pl.semaphore_wait(barrier, jnp.where(is_first | is_last, lon_size + 1, lon_size + 3))
+    around = RUN + steps - 2 + jnp.where(at_start | at_end, 1, 0)
+    greetings = jnp.where(is_last, lon_size + 1, around + jnp.where(is_first, 2, 4))
+    pl.semaphore_wait(barrier, greetings)
 
     @pl.when(before_last)
     def _():
@@ -291,11 +318,11 @@
             bias_recv.at[one_if_last, lon],
             bias_send.at[s],
             bias_rsem.at[one_if_last, lon],
-            (below, lax.rem(lon + s, lon_size)),
+            (below, run_peer(s)),
         )
 
     def bias_arrival(slot, s):
-        source = lax.rem(lon + s, lon_size)
+        source = run_peer(s)
         return remote(
             bias_msg,
             bias_recv.at[slot, source],
@@ -304,6 +331,23 @@
             (dn, lon),
         )
 
+    def bias_pass(slot, s):
+        mine = bias_recv.at[slot, pl.ds(column * RUN, RUN)]
+        return remote(
+            mine,
+            mine,
+            pass_send.at[slot, s],
+            pass_recv.at[slot, column],
+            (lat, column_peer(s) * RUN + inside),
+        )
+
+    def bias_passed(slot, s):
+        source = column_peer(s)
+        theirs = bias_recv.at[slot, pl.ds(source * RUN, RUN)]
+        return remote(
+            theirs, theirs, pass_send.at[slot, s], pass_recv.at[slot, source], (dn, lon)
+        )
+
     def send_bias(s, carry):
         bias_copy(s).start()
         return carry
@@ -323,7 +367,7 @@
         def _():
             small_top(kind).start()
 
-    lax.fori_loop(1 - one_if_last, lon_size, send_bias, 0)
+    lax.fori_loop(1 - one_if_last, RUN, send_bias, 0)
     send_halo(0)
     loads[2].wait()
     pack_in(c_in, 1)
@@ -397,27 +441,54 @@
         back_copy_big(kind, slot).start()
         back_big[kind, slot] = res_big[kind, slot, slot]
 
+    def table_pass(slot, s):
+        target = column_peer(s)
+        return remote(
+            table_msg.at[slot, pl.ds(target * RUN, RUN)],
+            table_mid.at[slot, column],
+            table_xsend.at[slot, s],
+            table_xrecv.at[slot, column],
+            (lat, target * RUN + inside),
+        )
+
+    def table_passed(slot, s):
+        source = column_peer(s)
+        return remote(
+            table_msg.at[slot, pl.ds(source * RUN, RUN)],
+            table_mid.at[slot, source],
+            table_xsend.at[slot, s],
+            table_xrecv.at[slot, source],
+            (lat, lon),
+        )
+
     def table_copy(slot, s):
-        peer = lax.rem(lon + s, lon_size)
-        return remote(
-            table_msg.at[slot, peer],
-            table_recv.at[lon],
+        peer = lax.rem(inside + s, RUN)
+        return remote(
+            table_out.at[slot, peer],
+            table_recv.at[inside],
             table_send.at[slot, s],
-            table_rsem.at[lon],
-            (jnp.where(slot == 0, lat, up), peer),
+            table_rsem.at[inside],
+            (jnp.where(slot == 0, lat, up), run_peer(s)),
         )
 
     def table_arrival(s):
-        source = lax.rem(lon + s, lon_size)
-        return remote(
-            table_msg.at[0, source],
+        source = lax.rem(inside + s, RUN)
+        return remote(
+            table_out.at[0, source],
             table_recv.at[source],
             table_send.at[0, s],
             table_rsem.at[source],
-            (lat, source),
+            (lat, run_peer(s)),
         )
 
     def window_row(slot, carry):
+        def wait_bias(s, inner):
+            bias_arrival(slot, s).wait_recv()
+            return inner
+
+        lax.fori_loop(1 - slot, RUN, wait_bias, 0)
+        for s in range(1, steps):
+            bias_pass(slot, s).start()
         gain = gain_ref[...]
         wait_halo(0, slot)
         unpack_in(0, slot)
@@ -452,11 +523,8 @@
             real = jnp.where(key_band == a, pad_ref[lax.rem(first_row + a, total_rows)], real)
         allowed = (jnp.abs(query_row - key_row) < WIN_LAT) & (real == 1)
 
-        def wait_bias(s, inner):
-            bias_arrival(slot, s).wait_recv()
-            return inner
-
-        lax.fori_loop(1 - slot, lon_size, wait_bias, 0)
+        for s in range(1, steps):
+            bias_passed(slot, s).wait_recv()
         for p in range(PAIRS):
             owner, r = p // pairs_here, p % pairs_here
             zq, zt = p // ZONE, p % ZONE
@@ -561,16 +629,8 @@
                 zt * 8 : zt * 8 + 8, zq * SLOT : (zq + 1) * SLOT
             ]
 
-        def send_table(s, inner):
-            table_copy(slot, s).start()
-            return inner
-
-        lax.fori_loop(1 - slot, lon_size, send_table, 0)
-
-        @pl.when(slot == 0)
-        def _():
-            table_recv[lon] = table_msg[0, lon]
-
+        for s in range(1, steps):
+            table_pass(slot, s).start()
         return carry
 
     rows_here = 1 + one_if_first - one_if_last
@@ -614,6 +674,27 @@
         for r in range(WIN_LAT):
             dst[r] = raw[r * COLS : (r + 1) * COLS, :].astype(BF16)
 
+    def table_row(slot, carry):
+        summed = table_msg[slot, pl.ds(column * RUN, RUN)]
+        for s in range(1, steps):
+            table_passed(slot, s).wait_recv()
+        for s in range(1, steps):
+            summed = summed + table_mid[slot, column_peer(s)]
+        table_out[slot] = summed
+
+        def send_table(s, inner):
+            table_copy(slot, s).start()
+            return inner
+
+        lax.fori_loop(1 - slot, RUN, send_table, 0)
+
+        @pl.when(slot == 0)
+        def _():
+            table_recv[inside] = table_out[0, inside]
+
+        return carry
+
+    lax.fori_loop(0, rows_here, table_row, 0)
     take_back(0, out_ref)
     take_back(1, grads_ref)
 
@@ -621,9 +702,9 @@
         table_arrival(s).wait_recv()
         return carry
 
-    lax.fori_loop(1 - one_if_last, lon_size, wait_table, 0)
+    lax.fori_loop(1 - one_if_last, RUN, wait_table, 0)
     added = table_recv[0]
-    for j in range(1, lon_size):
+    for j in range(1, RUN):
         added = added + table_recv[j]
     for r in range(pairs_here):
         piece = added[:, r * SLOT : r * SLOT + OFFSETS]
@@ -647,7 +728,7 @@
         bias_copy(s).wait_send()
         return carry
 
-    lax.fori_loop(1 - one_if_last, lon_size, drain_bias, 0)
+    lax.fori_loop(1 - one_if_last, RUN, drain_bias, 0)
 
     def drain_row(slot, carry):
         for kind in range(2):
@@ -659,7 +740,10 @@
             table_copy(slot, s).wait_send()
             return inner
 
-        lax.fori_loop(1 - slot, lon_size, drain_table, 0)
+        lax.fori_loop(1 - slot, RUN, drain_table, 0)
+        for s in range(1, steps):
+            bias_pass(slot, s).wait_send()
+            table_pass(slot, s).wait_send()
         return carry
 
     lax.fori_loop(0, rows_here, drain_row, 0)
@@ -732,7 +816,9 @@
                 pltpu.VMEM((2, TOKENS * 8, 128), F32),
                 pltpu.VMEM((WINDOWS * CELLS, FEATS), F32),
                 pltpu.VMEM((2, lon_size, 8, lanes), F32),
-                pltpu.VMEM((lon_size, 8, lanes), F32),
+                pltpu.VMEM((2, lon_size // RUN, RUN, 8, lanes), F32),
+                pltpu.VMEM((2, RUN, 8, lanes), F32),
+                pltpu.VMEM((RUN, 8, lanes), F32),
                 pltpu.VMEM((WIN_LON, BAND, TOKENS), BF16),
                 pltpu.VMEM((WIN_LON, TOKENS, BAND), BF16),
                 pltpu.VMEM((WINDOWS, HEADS, TOKENS, TOKENS), F32),
@@ -744,10 +830,14 @@
                 pltpu.SemaphoreType.DMA((2, 2, 3)),
                 pltpu.SemaphoreType.DMA((2, 2, 3)),
                 pltpu.SemaphoreType.DMA((2, 4)),
-                pltpu.SemaphoreType.DMA((lon_size,)),
+                pltpu.SemaphoreType.DMA((RUN,)),
                 pltpu.SemaphoreType.DMA((2, lon_size)),
-                pltpu.SemaphoreType.DMA((2, lon_size)),
-                pltpu.SemaphoreType.DMA((lon_size,)),
+                pltpu.SemaphoreType.DMA((2, lon_size // RUN)),
+                pltpu.SemaphoreType.DMA((2, lon_size // RUN)),
+                pltpu.SemaphoreType.DMA((2, lon_size // RUN)),
+                pltpu.SemaphoreType.DMA((2, lon_size // RUN)),
+                pltpu.SemaphoreType.DMA((2, RUN)),
+                pltpu.SemaphoreType.DMA((RUN,)),
                 pltpu.SemaphoreType.REGULAR,
             ],
             compiler_params=pltpu.CompilerParams(

time: 41.4 us -> 42.3 us (1.022)
  Pallas kernels: 40.6 us -> 41.1 us
    pallas_call x1, Pallas kernels: 39.9 us -> 40.4 us  [per_device(): pl.pallas_call(functools.partial(kernel, lat_size, lon_size, pairs_here),...]
where the time goes in v4:
time: 42.3 us; the launch traced here: 41.8 us
  Pallas kernels  41.1 us (97%)
  between operations  0.64 us (2%)
    pallas_call x1, Pallas kernels, per_device(): pl.pallas_call(functools.partial(kernel, lat_size, lon_size, pairs_here),...  40.4 us

profile of v4, /device:TPU:6, one launch (start us, length us, event | category | flops | bytes accessed | tf_op | source)
XLA Modules:
  0.0 41.8 jit_solution(18249450858304932801)
XLA Ops:
  0.6 40.4 %shard_map.94 = (bf16[6,24,384]{2,1,0:T(8,128)(2,1)S(1)}, bf16[6,24,384]{2,1,0:T(8,128)(2,1)S(1)}, f32[6,9,1,23]{3,2,1,0:T(1,128)S(1)}) custom-call(bf16[6,24,384]{2,1,0:T(8,128)(2,1)} %fields_hbm.1, f32[1,192]{1,0:T(1,128)} %bitcast.4, bf16[192,576]{1,0:T(8,128)(2,1)} %win_hbm.1, bf16[192,192]{1,0:T(8,128)(2,1)} %wout_hbm.1, f32[6,9,1,23]{3,2,1,0:T(1,128)} %bitcast.3, ...), custom_call_target="tpu_custom_call" | custom-call | tf_op jit(solution)/shard_map/pallas_call | solution.py:772
  41.0 0.7 %shard_map.95 = (bf16[6,24,384]{2,1,0:T(8,128)(2,1)}, bf16[6,24,384]{2,1,0:T(8,128)(2,1)}, f32[6,9,1,23]{3,2,1,0:T(1,128)}) custom-call(bf16[6,24,384]{2,1,0:T(8,128)(2,1)S(1)} %get-tuple-element.9.refs_0_, bf16[6,24,384]{2,1,0:T(8,128)(2,1)S(1)} %get-tuple-element.10.refs_1_, f32[6,9,1,23]{3,2,1,0:T(1,128)S(1)} %get-tuple-element.11.refs_2_), custom_call_target="tpu_custom_call" | custom-call | tf_op jit(solution)/shard_map/pallas_call | solution.py:862

commit v5 on v4

--- a/solution.py
+++ b/solution.py
@@ -135,14 +135,18 @@
     is_last = place == group - 1
     before_last = place == group - 2
     one_if_last = jnp.where(is_last, 1, 0)
+    is_helper = place == 1
     one_if_first = jnp.where(is_first, 1, 0)
+    one_if_helper = jnp.where(is_helper, 1, 0)
+    helper = lax.rem(lat + 2, lat_size)
+    helped = lax.rem(lat + lat_size - 2, lat_size)
     steps = lon_size // RUN
     column = lon // RUN
     inside = lax.rem(lon, RUN)
     at_start = inside == 0
     at_end = inside == RUN - 1
-    below = jnp.where(is_last, dn, lat)
-    above = jnp.where(is_first, lat, up)
+    below = jnp.where(is_last, helper, lat)
+    above = jnp.where(is_first, dn, up)
 
     barrier = pltpu.get_barrier_semaphore()
 
@@ -150,7 +154,7 @@
         pl.semaphore_signal(barrier, inc=1, device_id=dev, device_id_type=MESH)
 
     def greet_seam(s, carry):
-        signal((up, lax.rem(lon + s, lon_size)))
+        signal((helped, lax.rem(lon + s, lon_size)))
         return carry
 
     def run_peer(s):
@@ -159,9 +163,14 @@
     def column_peer(s):
         return lax.rem(column + s, steps)
 
+    @pl.when(is_helper)
+    def _():
+        signal((up, rt))
+        lax.fori_loop(0, lon_size, greet_seam, 0)
+
     @pl.when(is_first)
     def _():
-        lax.fori_loop(0, lon_size, greet_seam, 0)
+        signal((dn, lf))
 
     @pl.when(jnp.logical_not(is_first))
     def _():
@@ -221,16 +230,16 @@
             in_big.at[kind, 1, 0],
             halo_send.at[kind, 0],
             halo_recv.at[kind, 1, 0],
-            (dn, lon),
-        )
-
-    def big_up(kind):
+            (helper, lon),
+        )
+
+    def big_top(kind):
         return remote(
             send_big.at[kind, 1],
-            in_big.at[kind, 0, 1],
+            in_big.at[kind, one_if_first, 1],
             halo_send.at[kind, 1],
-            halo_recv.at[kind, 0, 0],
-            (up, lon),
+            halo_recv.at[kind, one_if_first, 1],
+            (above, lon),
         )
 
     def small_low(kind):
@@ -238,7 +247,7 @@
             send_small.at[kind, 0],
             in_small.at[kind, one_if_last, 0],
             halo_send.at[kind, 2],
-            halo_recv.at[kind, one_if_last, 1],
+            halo_recv.at[kind, one_if_last, 2],
             (below, lf),
         )
 
@@ -247,24 +256,28 @@
             send_small.at[kind, 1],
             in_small.at[kind, one_if_first, 1],
             halo_send.at[kind, 3],
-            halo_recv.at[kind, one_if_first, 2],
+            halo_recv.at[kind, one_if_first, 3],
             (above, lf),
         )
 
     def wait_halo(kind, slot):
-        remote(
-            send_big.at[kind, 0],
-            in_big.at[kind, slot, 1 - slot],
-            halo_send.at[kind, 0],
-            halo_recv.at[kind, slot, 0],
-            (dn, lon),
-        ).wait_recv()
+        def arrived_big(half, carry):
+            remote(
+                send_big.at[kind, 0],
+                in_big.at[kind, slot, half],
+                halo_send.at[kind, 0],
+                halo_recv.at[kind, slot, half],
+                (dn, lon),
+            ).wait_recv()
+            return carry
+
+        lax.fori_loop(1 - slot, 2, arrived_big, 0)
         for half in range(2):
             remote(
                 send_small.at[kind, half],
                 in_small.at[kind, slot, half],
                 halo_send.at[kind, 2],
-                halo_recv.at[kind, slot, 1 + half],
+                halo_recv.at[kind, slot, 2 + half],
                 (dn, lon),
             ).wait_recv()
 
@@ -280,7 +293,8 @@
                 tmp[side + r * 6 : side + 6 + r * 6, :] = raw[row : row + 6, :]
             piece = tmp[base : base + BIG, :].astype(BF16)
             send_big[kind, half] = piece
-            in_big[kind, half, half] = piece
+            if half == 0:
+                in_big[kind, 0, 0] = piece
             send_small[kind, half] = tmp[side : side + SMALL, :].astype(BF16)
 
     def unpack_in(kind, slot):
@@ -305,7 +319,9 @@
     pack_in(f_in, 0)
 
     around = RUN + steps - 2 + jnp.where(at_start | at_end, 1, 0)
-    greetings = jnp.where(is_last, lon_size + 1, around + jnp.where(is_first, 2, 4))
+    greetings = jnp.where(
+        is_last, lon_size + 1, around + jnp.where(is_first, 3, 4 + one_if_helper)
+    )
     pl.semaphore_wait(barrier, greetings)
 
     @pl.when(before_last)
@@ -359,9 +375,7 @@
 
         small_low(kind).start()
 
-        @pl.when(jnp.logical_not(is_first))
-        def _():
-            big_up(kind).start()
+        big_top(kind).start()
 
         @pl.when(jnp.logical_not(is_last))
         def _():
@@ -404,23 +418,25 @@
     key_band = (lax.broadcasted_iota(jnp.int32, (TOKENS, TOKENS), 0) // WIN_LON) % WIN_LAT
     query_band = (lax.broadcasted_iota(jnp.int32, (TOKENS, TOKENS), 1) // WIN_LON) % WIN_LAT
 
-    def back_copy_big(kind, slot):
-        return remote(
-            res_big.at[kind, slot, 1 - slot],
-            back_big.at[kind, 1 - slot],
-            back_send.at[kind, slot, 0],
-            back_recv.at[kind, 1 - slot],
-            (jnp.where(slot == 0, dn, up), lon),
+    def owner_of(slot, half):
+        return lax.rem(lat + half - 2 * slot + lat_size, lat_size)
+
+    def back_copy_big(kind, slot, half):
+        return remote(
+            res_big.at[kind, slot, half],
+            back_big.at[kind, half],
+            back_send.at[kind, slot, half],
+            back_recv.at[kind, half],
+            (owner_of(slot, half), lon),
         )
 
     def back_copy_small(kind, slot, half):
-        owner = lax.rem(lat + half - slot + lat_size, lat_size)
         return remote(
             res_small.at[kind, slot, half],
             back_small.at[kind, half],
-            back_send.at[kind, slot, 1 + half],
+            back_send.at[kind, slot, 2 + half],
             back_recv.at[kind, 2 + half],
-            (owner, rt),
+            (owner_of(slot, half), rt),
         )
 
     def give_back(kind, slot, tokens):
@@ -438,8 +454,15 @@
             res_small[kind, slot, half] = tmp[side : side + SMALL, :].astype(BF16)
         for half in range(2):
             back_copy_small(kind, slot, half).start()
-        back_copy_big(kind, slot).start()
-        back_big[kind, slot] = res_big[kind, slot, slot]
+        back_copy_big(kind, slot, 1).start()
+
+        @pl.when(slot == 1)
+        def _():
+            back_copy_big(kind, slot, 0).start()
+
+        @pl.when(slot == 0)
+        def _():
+            back_big[kind, 0] = res_big[kind, 0, 0]
 
     def table_pass(slot, s):
         target = column_peer(s)
@@ -468,7 +491,7 @@
             table_recv.at[inside],
             table_send.at[slot, s],
             table_rsem.at[inside],
-            (jnp.where(slot == 0, lat, up), run_peer(s)),
+            (jnp.where(slot == 0, lat, helped), run_peer(s)),
         )
 
     def table_arrival(s):
@@ -481,7 +504,31 @@
             (lat, run_peer(s)),
         )
 
+    def table_row(slot, carry):
+        summed = table_msg[slot, pl.ds(column * RUN, RUN)]
+        for s in range(1, steps):
+            table_passed(slot, s).wait_recv()
+        for s in range(1, steps):
+            summed = summed + table_mid[slot, column_peer(s)]
+        table_out[slot] = summed
+
+        def send_table(s, inner):
+            table_copy(slot, s).start()
+            return inner
+
+        lax.fori_loop(1 - slot, RUN, send_table, 0)
+
+        @pl.when(slot == 0)
+        def _():
+            table_recv[inside] = table_out[0, inside]
+
+        return carry
+
     def window_row(slot, carry):
+        @pl.when(slot == 1)
+        def _():
+            table_row(0, 0)
+
         def wait_bias(s, inner):
             bias_arrival(slot, s).wait_recv()
             return inner
@@ -515,7 +562,7 @@
             ctok[w] = c
             gmix_t[w] = dot_nt(wo_in[...], c.astype(BF16)).astype(BF16)
 
-        first_row = jnp.where(slot == 0, lat, up) * WIN_LAT + RIM_R
+        first_row = jnp.where(slot == 0, lat, helped) * WIN_LAT + RIM_R
         key_row = lax.rem(first_row + key_band, total_rows)
         query_row = lax.rem(first_row + query_band, total_rows)
         real = jnp.zeros((TOKENS, TOKENS), jnp.int32)
@@ -633,7 +680,7 @@
             table_pass(slot, s).start()
         return carry
 
-    rows_here = 1 + one_if_first - one_if_last
+    rows_here = 1 + one_if_helper - one_if_last
     lax.fori_loop(0, rows_here, window_row, 0)
 
     def take_back(kind, dst):
@@ -650,10 +697,7 @@
         def _():
             arrived_big(0)
 
-        @pl.when(jnp.logical_not(is_first))
-        def _():
-            arrived_big(1)
-
+        arrived_big(1)
         for half in range(2):
             remote(
                 res_small.at[kind, 0, half],
@@ -674,28 +718,8 @@
         for r in range(WIN_LAT):
             dst[r] = raw[r * COLS : (r + 1) * COLS, :].astype(BF16)
 
-    def table_row(slot, carry):
-        summed = table_msg[slot, pl.ds(column * RUN, RUN)]
-        for s in range(1, steps):
-            table_passed(slot, s).wait_recv()
-        for s in range(1, steps):
-            summed = summed + table_mid[slot, column_peer(s)]
-        table_out[slot] = summed
-
-        def send_table(s, inner):
-            table_copy(slot, s).start()
-            return inner
-
-        lax.fori_loop(1 - slot, RUN, send_table, 0)
-
-        @pl.when(slot == 0)
-        def _():
-            table_recv[inside] = table_out[0, inside]
-
-        return carry
-
-    lax.fori_loop(0, rows_here, table_row, 0)
     take_back(0, out_ref)
+    lax.fori_loop(jnp.maximum(rows_here - 1, 0), rows_here, table_row, 0)
     take_back(1, grads_ref)
 
     def wait_table(s, carry):
@@ -717,10 +741,7 @@
         def _():
             big_last(kind).wait_send()
 
-        @pl.when(jnp.logical_not(is_first))
-        def _():
-            big_up(kind).wait_send()
-
+        big_top(kind).wait_send()
         small_low(kind).wait_send()
         small_top(kind).wait_send()
 
@@ -732,7 +753,12 @@
 
     def drain_row(slot, carry):
         for kind in range(2):
-            back_copy_big(kind, slot).wait_send()
+            back_copy_big(kind, slot, 1).wait_send()
+
+            @pl.when(slot == 1)
+            def _():
+                back_copy_big(kind, slot, 0).wait_send()
+
             for half in range(2):
                 back_copy_small(kind, slot, half).wait_send()
 
@@ -827,8 +853,8 @@
                 pltpu.VMEM((WINDOWS, HEADS, TOKENS, TOKENS), BF16),
                 pltpu.SemaphoreType.DMA((7,)),
                 pltpu.SemaphoreType.DMA((2, 4)),
-                pltpu.SemaphoreType.DMA((2, 2, 3)),
-                pltpu.SemaphoreType.DMA((2, 2, 3)),
+                pltpu.SemaphoreType.DMA((2, 2, 4)),
+                pltpu.SemaphoreType.DMA((2, 2, 4)),
                 pltpu.SemaphoreType.DMA((2, 4)),
                 pltpu.SemaphoreType.DMA((RUN,)),
                 pltpu.SemaphoreType.DMA((2, lon_size)),

time: 42.3 us -> 43.3 us (1.024)
  the two profiles are of different devices: /device:TPU:6 before, /device:TPU:1 now
where the time goes in v5:
time: 43.3 us; the launch traced here: 43.1 us
  Pallas kernels  42.5 us (98%)
  between operations  0.64 us (1%)
    pallas_call x1, Pallas kernels, per_device(): pl.pallas_call(functools.partial(kernel, lat_size, lon_size, pairs_here),...  41.8 us

profile of v5, /device:TPU:1, one launch (start us, length us, event | category | flops | bytes accessed | tf_op | source)
XLA Modules:
  0.0 43.1 jit_solution(2916242462663940632)
XLA Ops:
  0.6 41.8 %shard_map.94 = (bf16[6,24,384]{2,1,0:T(8,128)(2,1)S(1)}, bf16[6,24,384]{2,1,0:T(8,128)(2,1)S(1)}, f32[6,9,1,23]{3,2,1,0:T(1,128)S(1)}) custom-call(bf16[6,24,384]{2,1,0:T(8,128)(2,1)} %fields_hbm.1, f32[1,192]{1,0:T(1,128)} %bitcast.4, bf16[192,576]{1,0:T(8,128)(2,1)} %win_hbm.1, bf16[192,192]{1,0:T(8,128)(2,1)} %wout_hbm.1, f32[6,9,1,23]{3,2,1,0:T(1,128)} %bitcast.3, ...), custom_call_target="tpu_custom_call" | custom-call | tf_op jit(solution)/shard_map/pallas_call | solution.py:798
  42.4 0.7 %shard_map.95 = (bf16[6,24,384]{2,1,0:T(8,128)(2,1)}, bf16[6,24,384]{2,1,0:T(8,128)(2,1)}, f32[6,9,1,23]{3,2,1,0:T(1,128)}) custom-call(bf16[6,24,384]{2,1,0:T(8,128)(2,1)S(1)} %get-tuple-element.9.refs_0_, bf16[6,24,384]{2,1,0:T(8,128)(2,1)S(1)} %get-tuple-element.10.refs_1_, f32[6,9,1,23]{3,2,1,0:T(1,128)S(1)} %get-tuple-element.11.refs_2_), custom_call_target="tpu_custom_call" | custom-call | tf_op jit(solution)/shard_map/pallas_call | solution.py:888

commit v6 on v4

--- a/solution.py
+++ b/solution.py
@@ -121,7 +121,9 @@
     table_xrecv,
     table_send,
     table_rsem,
+    far_send,
     ready_sem,
+    alive_sem,
 ):
     lat = lax.axis_index("lat")
     lon = lax.axis_index("lon")
@@ -301,9 +303,6 @@
         for h in range(HEADS):
             bias_msg[h : h + 1, r * SLOT : r * SLOT + OFFSETS] = bias_in[h, r]
     bias_recv[0, lon] = bias_msg[...]
-    loads[1].wait()
-    pack_in(f_in, 0)
-
     around = RUN + steps - 2 + jnp.where(at_start | at_end, 1, 0)
     greetings = jnp.where(is_last, lon_size + 1, around + jnp.where(is_first, 2, 4))
     pl.semaphore_wait(barrier, greetings)
@@ -368,13 +367,20 @@
             small_top(kind).start()
 
     lax.fori_loop(1 - one_if_last, RUN, send_bias, 0)
+    loads[1].wait()
+    pack_in(f_in, 0)
     send_halo(0)
     loads[2].wait()
     pack_in(c_in, 1)
     send_halo(1)
 
+    def say_alive(j, carry):
+        pl.semaphore_signal(alive_sem, inc=1, device_id=(dn, j), device_id_type=MESH)
+        return carry
+
     @pl.when(is_last)
     def _():
+        lax.fori_loop(0, lon_size, say_alive, 0)
         pl.semaphore_wait(ready_sem, 1)
         for kind in range(2):
             small_top(kind).start()
@@ -468,7 +474,7 @@
             table_recv.at[inside],
             table_send.at[slot, s],
             table_rsem.at[inside],
-            (jnp.where(slot == 0, lat, up), run_peer(s)),
+            (lat, run_peer(s)),
         )
 
     def table_arrival(s):
@@ -480,6 +486,30 @@
             table_rsem.at[source],
             (lat, run_peer(s)),
         )
+
+    def table_far(j):
+        return remote(
+            table_msg.at[1, j],
+            table_recv.at[lon],
+            far_send.at[j],
+            table_rsem.at[lon],
+            (up, j),
+        )
+
+    def near_table():
+        summed = table_msg[0, pl.ds(column * RUN, RUN)]
+        for s in range(1, steps):
+            table_passed(0, s).wait_recv()
+        for s in range(1, steps):
+            summed = summed + table_mid[0, column_peer(s)]
+        table_out[0] = summed
+
+        def send_table(s, inner):
+            table_copy(0, s).start()
+            return inner
+
+        lax.fori_loop(1, RUN, send_table, 0)
+        table_recv[inside] = table_out[0, inside]
 
     def window_row(slot, carry):
         def wait_bias(s, inner):
@@ -515,6 +545,13 @@
             ctok[w] = c
             gmix_t[w] = dot_nt(wo_in[...], c.astype(BF16)).astype(BF16)
 
+        def rows_of(part, h):
+            return pl.ds(part * WIDTH + h * HEAD_DIM, HEAD_DIM)
+
+        for h in range(HEADS):
+            for w in range(WINDOWS):
+                score_buf[w, h] = dot_nn(k_nat[w, h], proj_t[w, rows_of(0, h), :]) * SCALE
+                gw_buf[w, h] = dot_nn(v_nat[w, h], gmix_t[w, rows_of(0, h), :])
         first_row = jnp.where(slot == 0, lat, up) * WIN_LAT + RIM_R
         key_row = lax.rem(first_row + key_band, total_rows)
         query_row = lax.rem(first_row + query_band, total_rows)
@@ -522,6 +559,10 @@
         for a in range(WIN_LAT):
             real = jnp.where(key_band == a, pad_ref[lax.rem(first_row + a, total_rows)], real)
         allowed = (jnp.abs(query_row - key_row) < WIN_LAT) & (real == 1)
+
+        @pl.when(slot == 1)
+        def _():
+            near_table()
 
         for s in range(1, steps):
             bias_passed(slot, s).wait_recv()
@@ -553,19 +594,10 @@
             whole = jnp.concatenate([left, right[:, 0 : TOKENS - 128]], axis=1)
             bias_full[h] = jnp.where(allowed, whole, MASKED)
 
-        def rows_of(part, h):
-            return pl.ds(part * WIDTH + h * HEAD_DIM, HEAD_DIM)
-
-        for h in range(HEADS):
-            for w in range(WINDOWS):
-                score_buf[w, h] = (
-                    dot_nn(k_nat[w, h], proj_t[w, rows_of(0, h), :]) * SCALE + bias_full[h]
-                )
-                gw_buf[w, h] = dot_nn(v_nat[w, h], gmix_t[w, rows_of(0, h), :])
         for h in range(HEADS):
             summed = None
             for w in range(WINDOWS):
-                scores = score_buf[w, h]
+                scores = score_buf[w, h] + bias_full[h]
                 raised = jnp.exp(scores - jnp.max(scores, axis=0, keepdims=True))
                 weights = raised * (1.0 / jnp.sum(raised, axis=0, keepdims=True))
                 p_low[w, h] = weights.astype(BF16)
@@ -629,8 +661,21 @@
                 zt * 8 : zt * 8 + 8, zq * SLOT : (zq + 1) * SLOT
             ]
 
-        for s in range(1, steps):
-            table_pass(slot, s).start()
+        @pl.when(slot == 0)
+        def _():
+            for s in range(1, steps):
+                table_pass(0, s).start()
+
+        @pl.when(slot == 1)
+        def _():
+            pl.semaphore_wait(alive_sem, lon_size)
+
+            def send_far(j, inner):
+                table_far(j).start()
+                return inner
+
+            lax.fori_loop(0, lon_size, send_far, 0)
+
         return carry
 
     rows_here = 1 + one_if_first - one_if_last
@@ -674,27 +719,10 @@
         for r in range(WIN_LAT):
             dst[r] = raw[r * COLS : (r + 1) * COLS, :].astype(BF16)
 
-    def table_row(slot, carry):
-        summed = table_msg[slot, pl.ds(column * RUN, RUN)]
-        for s in range(1, steps):
-            table_passed(slot, s).wait_recv()
-        for s in range(1, steps):
-            summed = summed + table_mid[slot, column_peer(s)]
-        table_out[slot] = summed
-
-        def send_table(s, inner):
-            table_copy(slot, s).start()
-            return inner
-
-        lax.fori_loop(1 - slot, RUN, send_table, 0)
-
-        @pl.when(slot == 0)
-        def _():
-            table_recv[inside] = table_out[0, inside]
-
-        return carry
-
-    lax.fori_loop(0, rows_here, table_row, 0)
+    @pl.when(jnp.logical_not(is_first | is_last))
+    def _():
+        near_table()
+
     take_back(0, out_ref)
     take_back(1, grads_ref)
 
@@ -702,9 +730,27 @@
         table_arrival(s).wait_recv()
         return carry
 
-    lax.fori_loop(1 - one_if_last, RUN, wait_table, 0)
+    def wait_far(j, carry):
+        remote(
+            table_msg.at[1, j],
+            table_recv.at[j],
+            far_send.at[j],
+            table_rsem.at[j],
+            (up, j),
+        ).wait_recv()
+        return carry
+
+    @pl.when(is_last)
+    def _():
+        lax.fori_loop(0, lon_size, wait_far, 0)
+
+    @pl.when(jnp.logical_not(is_last))
+    def _():
+        lax.fori_loop(1, RUN, wait_table, 0)
+        table_recv[RUN:lon_size] = jnp.zeros_like(table_recv[RUN:lon_size])
+
     added = table_recv[0]
-    for j in range(1, RUN):
+    for j in range(1, lon_size):
         added = added + table_recv[j]
     for r in range(pairs_here):
         piece = added[:, r * SLOT : r * SLOT + OFFSETS]
@@ -736,14 +782,24 @@
             for half in range(2):
                 back_copy_small(kind, slot, half).wait_send()
 
-        def drain_table(s, inner):
-            table_copy(slot, s).wait_send()
-            return inner
-
-        lax.fori_loop(1 - slot, RUN, drain_table, 0)
         for s in range(1, steps):
             bias_pass(slot, s).wait_send()
-            table_pass(slot, s).wait_send()
+
+        @pl.when(slot == 0)
+        def _():
+            for s in range(1, steps):
+                table_pass(0, s).wait_send()
+            for s in range(1, RUN):
+                table_copy(0, s).wait_send()
+
+        @pl.when(slot == 1)
+        def _():
+            def drain_far(j, inner):
+                table_far(j).wait_send()
+                return inner
+
+            lax.fori_loop(0, lon_size, drain_far, 0)
+
         return carry
 
     lax.fori_loop(0, rows_here, drain_row, 0)
@@ -818,7 +874,7 @@
                 pltpu.VMEM((2, lon_size, 8, lanes), F32),
                 pltpu.VMEM((2, lon_size // RUN, RUN, 8, lanes), F32),
                 pltpu.VMEM((2, RUN, 8, lanes), F32),
-                pltpu.VMEM((RUN, 8, lanes), F32),
+                pltpu.VMEM((lon_size, 8, lanes), F32),
                 pltpu.VMEM((WIN_LON, BAND, TOKENS), BF16),
                 pltpu.VMEM((WIN_LON, TOKENS, BAND), BF16),
                 pltpu.VMEM((WINDOWS, HEADS, TOKENS, TOKENS), F32),
@@ -837,7 +893,9 @@
                 pltpu.SemaphoreType.DMA((2, lon_size // RUN)),
                 pltpu.SemaphoreType.DMA((2, lon_size // RUN)),
                 pltpu.SemaphoreType.DMA((2, RUN)),
-                pltpu.SemaphoreType.DMA((RUN,)),
+                pltpu.SemaphoreType.DMA((lon_size,)),
+                pltpu.SemaphoreType.DMA((lon_size,)),
+                pltpu.SemaphoreType.REGULAR,
                 pltpu.SemaphoreType.REGULAR,
             ],
             compiler_params=pltpu.CompilerParams(

time: 42.3 us -> 39.8 us (0.941)
  the two profiles are of different devices: /device:TPU:6 before, /device:TPU:2 now
where the time goes in v6:
time: 39.8 us; the launch traced here: 39.6 us
  Pallas kernels  39 us (98%)
  between operations  0.64 us (2%)
    pallas_call x1, Pallas kernels, per_device(): pl.pallas_call(functools.partial(kernel, lat_size, lon_size, pairs_here),...  38.3 us

profile of v6, /device:TPU:2, one launch (start us, length us, event | category | flops | bytes accessed | tf_op | source)
XLA Modules:
  0.0 39.6 jit_solution(9522924567750011877)
XLA Ops:
  0.6 38.3 %shard_map.94 = (bf16[6,24,384]{2,1,0:T(8,128)(2,1)S(1)}, bf16[6,24,384]{2,1,0:T(8,128)(2,1)S(1)}, f32[6,9,1,23]{3,2,1,0:T(1,128)S(1)}) custom-call(bf16[6,24,384]{2,1,0:T(8,128)(2,1)} %fields_hbm.1, f32[1,192]{1,0:T(1,128)} %bitcast.4, bf16[192,576]{1,0:T(8,128)(2,1)} %win_hbm.1, bf16[192,192]{1,0:T(8,128)(2,1)} %wout_hbm.1, f32[6,9,1,23]{3,2,1,0:T(1,128)} %bitcast.3, ...), custom_call_target="tpu_custom_call" | custom-call | tf_op jit(solution)/shard_map/pallas_call | solution.py:828
  38.9 0.7 %shard_map.95 = (bf16[6,24,384]{2,1,0:T(8,128)(2,1)}, bf16[6,24,384]{2,1,0:T(8,128)(2,1)}, f32[6,9,1,23]{3,2,1,0:T(1,128)}) custom-call(bf16[6,24,384]{2,1,0:T(8,128)(2,1)S(1)} %get-tuple-element.9.refs_0_, bf16[6,24,384]{2,1,0:T(8,128)(2,1)S(1)} %get-tuple-element.10.refs_1_, f32[6,9,1,23]{3,2,1,0:T(1,128)S(1)} %get-tuple-element.11.refs_2_), custom_call_target="tpu_custom_call" | custom-call | tf_op jit(solution)/shard_map/pallas_call | solution.py:920

commit v7 on v6

--- a/solution.py
+++ b/solution.py
@@ -101,6 +101,8 @@
     table_msg,
     table_mid,
     table_out,
+    far_msg,
+    far_recv,
     table_recv,
     spreader,
     gatherer,
@@ -489,8 +491,8 @@
 
     def table_far(j):
         return remote(
-            table_msg.at[1, j],
-            table_recv.at[lon],
+            far_msg.at[j],
+            far_recv.at[lon],
             far_send.at[j],
             table_rsem.at[lon],
             (up, j),
@@ -559,10 +561,6 @@
         for a in range(WIN_LAT):
             real = jnp.where(key_band == a, pad_ref[lax.rem(first_row + a, total_rows)], real)
         allowed = (jnp.abs(query_row - key_row) < WIN_LAT) & (real == 1)
-
-        @pl.when(slot == 1)
-        def _():
-            near_table()
 
         for s in range(1, steps):
             bias_passed(slot, s).wait_recv()
@@ -607,6 +605,10 @@
                 summed = grad_s if summed is None else summed + grad_s
             gflat[0, pl.ds(h, TOKENS, stride=8), :] = summed[:, 0:128]
             gflat[1, pl.ds(h, TOKENS, stride=8), 0 : TOKENS - 128] = summed[:, 128:TOKENS]
+        @pl.when(slot == 1)
+        def _():
+            near_table()
+
         for h in range(HEADS):
             for w in range(WINDOWS):
                 q_t = proj_t[w, rows_of(0, h), :]
@@ -668,6 +670,7 @@
 
         @pl.when(slot == 1)
         def _():
+            far_msg[...] = table_msg[1].astype(BF16)
             pl.semaphore_wait(alive_sem, lon_size)
 
             def send_far(j, inner):
@@ -732,8 +735,8 @@
 
     def wait_far(j, carry):
         remote(
-            table_msg.at[1, j],
-            table_recv.at[j],
+            far_msg.at[j],
+            far_recv.at[j],
             far_send.at[j],
             table_rsem.at[j],
             (up, j),
@@ -743,6 +746,7 @@
     @pl.when(is_last)
     def _():
         lax.fori_loop(0, lon_size, wait_far, 0)
+        table_recv[...] = far_recv[...].astype(F32)
 
     @pl.when(jnp.logical_not(is_last))
     def _():
@@ -874,6 +878,8 @@
                 pltpu.VMEM((2, lon_size, 8, lanes), F32),
                 pltpu.VMEM((2, lon_size // RUN, RUN, 8, lanes), F32),
                 pltpu.VMEM((2, RUN, 8, lanes), F32),
+                pltpu.VMEM((lon_size, 8, lanes), BF16),
+                pltpu.VMEM((lon_size, 8, lanes), BF16),
                 pltpu.VMEM((lon_size, 8, lanes), F32),
                 pltpu.VMEM((WIN_LON, BAND, TOKENS), BF16),
                 pltpu.VMEM((WIN_LON, TOKENS, BAND), BF16),

time: 39.8 us -> 41 us (1.030)
  Pallas kernels: 39 us -> 40.2 us
    pallas_call x1, Pallas kernels: 38.3 us -> 39.5 us  [per_device(): pl.pallas_call(functools.partial(kernel, lat_size, lon_size, pairs_here),...]
where the time goes in v7:
time: 41 us; the launch traced here: 40.8 us
  Pallas kernels  40.2 us (98%)
  between operations  0.64 us (2%)
    pallas_call x1, Pallas kernels, per_device(): pl.pallas_call(functools.partial(kernel, lat_size, lon_size, pairs_here),...  39.5 us

profile of v7, /device:TPU:2, one launch (start us, length us, event | category | flops | bytes accessed | tf_op | source)
XLA Modules:
  0.0 40.8 jit_solution(16371555647840809064)
XLA Ops:
  0.6 39.5 %shard_map.94 = (bf16[6,24,384]{2,1,0:T(8,128)(2,1)S(1)}, bf16[6,24,384]{2,1,0:T(8,128)(2,1)S(1)}, f32[6,9,1,23]{3,2,1,0:T(1,128)S(1)}) custom-call(bf16[6,24,384]{2,1,0:T(8,128)(2,1)} %fields_hbm.1, f32[1,192]{1,0:T(1,128)} %bitcast.4, bf16[192,576]{1,0:T(8,128)(2,1)} %win_hbm.1, bf16[192,192]{1,0:T(8,128)(2,1)} %wout_hbm.1, f32[6,9,1,23]{3,2,1,0:T(1,128)} %bitcast.3, ...), custom_call_target="tpu_custom_call" | custom-call | tf_op jit(solution)/shard_map/pallas_call | solution.py:832
  40.1 0.7 %shard_map.95 = (bf16[6,24,384]{2,1,0:T(8,128)(2,1)}, bf16[6,24,384]{2,1,0:T(8,128)(2,1)}, f32[6,9,1,23]{3,2,1,0:T(1,128)}) custom-call(bf16[6,24,384]{2,1,0:T(8,128)(2,1)S(1)} %get-tuple-element.9.refs_0_, bf16[6,24,384]{2,1,0:T(8,128)(2,1)S(1)} %get-tuple-element.10.refs_1_, f32[6,9,1,23]{3,2,1,0:T(1,128)S(1)} %get-tuple-element.11.refs_2_), custom_call_target="tpu_custom_call" | custom-call | tf_op jit(solution)/shard_map/pallas_call | solution.py:926
